TPU v7x, 128 devices: a whole 4x4x4 slice. The times are simulated.
128 devices in a mesh: rep: 4 (over z_lo, core), shard: 32 (over y, z_hi, x).
Axes of the slice: x: 4, y: 4, z: 4 (z_hi: 2, z_lo: 2; z = z_hi * 2 + z_lo), core: 2. Of those that a mesh axis runs over, the one named last changes fastest.
Arguments:
- weight: bfloat16 [4, 32, 512, 2048], P('rep', None, 'shard'), may hold values from -3 to 3
- tracker: float32 [4, 32, 512, 2048], P('rep', None, 'shard'), may hold values from -40 to 40, as said below
- grad_new: bfloat16 [4, 32, 512, 2048], P('rep', None, 'shard'), may hold values from -6 to 6
- grad_old: bfloat16 [4, 32, 512, 2048], P('rep', None, 'shard'), may hold values from -6 to 6
- mix_keep: int32 [4, 2], replicated, may hold values from 4 to 12, as said below
Outputs:
- new_weight: bfloat16 [4, 32, 512, 2048], P('rep', None, 'shard')
- new_tracker: float32 [4, 32, 512, 2048], P('rep', None, 'shard')
- update: bfloat16 [4, 32, 512, 2048], P('rep', None, 'shard')
Inputs may be any that keep to these rules, and one draw needn't show every extreme that they name: `mix_keep`: every entry is one of the integers 4 to 12; some entry equals 4 and some equals 12. `tracker`: finite real values.
All inputs are finite; a program needn't handle non-finite values.
Results may differ from a plain program's by a relative error of at most 0.023.
Values may be sent and summed in bfloat16 or wider, within the bound.
A program may use at most 128 MiB of HBM per device.

v0:
```python
import math

import jax
import jax.numpy as jnp
from jax import lax
from jax.sharding import PartitionSpec as P

NS_STEPS = 5


coeff_a = 3.4445
coeff_b = -4.775
coeff_c = 2.0315
learn_rate = 0.05


def swapped(shard, axis, bit):
    return lax.ppermute(shard, axis, [(i, i ^ 1 << bit) for i in range(lax.axis_size(axis))])


def gossip_weight(values, keep_row):
    for bit_index in range(keep_row.shape[0]):
        partner = swapped(values, "rep", bit_index)
        own_share = keep_row[bit_index] / 16.0
        other_share = (16.0 - keep_row[bit_index]) / 16.0
        values = (
            own_share * values.astype(jnp.float32) + other_share * partner.astype(jnp.float32)
        ).astype(jnp.bfloat16)
    return values


def gossip_tracker(values, keep_row):
    for bit_index in range(keep_row.shape[0]):
        partner = swapped(values.astype(jnp.bfloat16), "rep", bit_index).astype(values.dtype)
        own_share = keep_row[bit_index] / 16.0
        other_share = (16.0 - keep_row[bit_index]) / 16.0
        values = own_share * values + other_share * partner
    return values


def orthogonalize(block_in):
    update_scale = 0.2 * math.sqrt(max(block_in.shape[1], block_in.shape[2]))
    values = block_in.astype(jnp.float32)
    frob_norm = jnp.sqrt(jnp.sum(values * values, axis=(1, 2), keepdims=True))
    iterate = (values / (frob_norm + 1e-07)).astype(jnp.bfloat16)
    for iteration in range(NS_STEPS):
        gram_matrix = jnp.einsum(
            "kmn,kpn->kmp", iterate, iterate, preferred_element_type=jnp.float32
        ).astype(jnp.bfloat16)
        square = jnp.einsum(
            "kmp,kpq->kmq", gram_matrix, gram_matrix, preferred_element_type=jnp.float32
        )
        polynomial = (coeff_b * gram_matrix.astype(jnp.float32) + coeff_c * square).astype(
            jnp.bfloat16
        )
        product = jnp.einsum(
            "kmp,kpn->kmn", polynomial, iterate, preferred_element_type=jnp.float32
        )
        iterate = (coeff_a * iterate.astype(jnp.float32) + product).astype(jnp.bfloat16)
    return (update_scale * iterate.astype(jnp.float32)).astype(jnp.bfloat16)


def settle(block_in):
    update_block = orthogonalize(block_in[0])[None]
    return lax.all_to_all(update_block, "shard", split_axis=2, concat_axis=0, tiled=True)


def local(weight, tracker, grad_new, grad_old, mix_keep):
    rep_index = lax.axis_index("rep")
    keep_all = mix_keep.astype(jnp.float32)
    keep_row = keep_all[rep_index]
    mixed_w = gossip_weight(weight, keep_row)
    mixed_y = gossip_tracker(tracker, keep_row)
    new_tracker = mixed_y + grad_new.astype(jnp.float32) - grad_old.astype(jnp.float32)
    rounded = new_tracker.astype(jnp.bfloat16)
    shards = lax.axis_size("shard")
    experts = rounded.shape[1]
    packed = rounded.reshape(shards, experts // shards, rounded.shape[2], rounded.shape[3])
    returned = settle(lax.all_to_all(packed, "shard", split_axis=0, concat_axis=2, tiled=True))
    update = returned.reshape(rounded.shape)
    new_weight = (mixed_w.astype(jnp.float32) - learn_rate * update.astype(jnp.float32)).astype(
        jnp.bfloat16
    )
    return (new_weight, new_tracker, update)


def solution(mesh):
    return jax.shard_map(
        local,
        mesh=mesh,
        in_specs=(
            P("rep", None, "shard", None),
            P("rep", None, "shard", None),
            P("rep", None, "shard", None),
            P("rep", None, "shard", None),
            P(),
        ),
        out_specs=(
            P("rep", None, "shard", None),
            P("rep", None, "shard", None),
            P("rep", None, "shard", None),
        ),
        check_vma=False,
    )
```

profile of v0, /device:TPU:0, one launch (start us, length us, event | category | flops | bytes accessed | tf_op | source)
XLA Modules:
  0.0 211.0 jit_solution(15291772610491671655)
XLA Ops:
  0.6 0.0 copy-start.5
  0.6 3.8 %convert_element_type.215 = bf16[1,32,16,2048]{3,2,1,0:T(8,128)(2,1)} convert(f32[1,32,16,2048]{3,2,1,0:T(8,128)} %param.6) | non-fusion elementwise | flops 1048576 | bytes 6291456 | tf_op jit(solution)/shard_map/convert_element_type | solution.py:34
  4.5 0.0 collective-permute-start.2
  4.5 0.0 copy-done.5
  4.5 0.1 constant_dynamic-slice_fusion
  4.6 0.5 fusion.34
  6.4 2.5 %collective-permute-done.2 = bf16[1,32,16,2048]{3,2,1,0:T(8,128)(2,1)S(1)} collective-permute-done((bf16[1,32,16,2048]{3,2,1,0:T(8,128)(2,1)}, bf16[1,32,16,2048]{3,2,1,0:T(8,128)(2,1)S(1)}, u32[]{:S(2)}, u32[]{:S(2)}) %collective-permute-start.2) | collective-permute-done | bytes 2097184 | tf_op jit(solution)/shard_map/ppermute | solution.py:18
  8.8 0.0 copy-start
  8.8 0.0 copy-start.2
  8.8 0.0 copy-start.3
  8.8 3.1 %fusion.3 = bf16[1,32,16,2048]{3,2,1,0:T(8,128)(2,1)S(1)} fusion(bf16[1,32,16,2048]{3,2,1,0:T(8,128)(2,1)S(1)} %collective-permute-done.2, f32[1,32,16,2048]{3,2,1,0:T(8,128)} %param.6, f32[]{:T(128)} %bitcast.2, f32[]{:T(128)} %bitcast.1), kind=kLoop, calls=%fused_computation.16 | loop fusion | flops 5242880 | bytes 8388616 | tf_op jit(solution)/shard_map/convert_element_type | solution.py:34
  11.9 2.1 collective-permute-start.3
  14.0 0.0 collective-permute-start
  15.3 44.6 %collective-permute-done.3 = bf16[1,32,16,2048]{3,2,1,0:T(8,128)(2,1)S(1)} collective-permute-done((bf16[1,32,16,2048]{3,2,1,0:T(8,128)(2,1)S(1)}, bf16[1,32,16,2048]{3,2,1,0:T(8,128)(2,1)S(1)}, u32[]{:S(2)}, u32[]{:S(2)}) %collective-permute-start.3) | collective-permute-done | bytes 2097184 | tf_op jit(solution)/shard_map/ppermute | solution.py:18
  60.0 0.0 copy-done
  60.0 0.0 copy-done.2
  60.0 0.0 copy-done.3
  60.0 4.9 %convert_bitcast_fusion = (bf16[32,1,16,2048]{3,2,1,0:T(8,128)(2,1)}, f32[1,32,16,2048]{3,2,1,0:T(8,128)}) fusion(bf16[1,32,16,2048]{3,2,1,0:T(8,128)(2,1)S(1)} %copy-done.2, bf16[1,32,16,2048]{3,2,1,0:T(8,128)(2,1)S(1)} %copy-done.3, bf16[1,32,16,2048]{3,2,1,0:T(8,128)(2,1)S(1)} %collective-permute-done.3, f32[]{:T(128)} %bitcast.3, ...), kind=kLoop, calls=%fused_computation.17 | loop fusion | flops 13631488 | bytes 18874384 | tf_op jit(solution)/shard_map/reshape | solution.py:78
  64.9 10.5 %all-to-all-start = ((bf16[32,1,16,2048]{3,2,1,0:T(8,128)(2,1)}), bf16[32,1,16,2048]{3,2,1,0:T(8,128)(2,1)S(1)}, u32[]{:S(2)}, u32[]{:S(2)}) async-start(bf16[32,1,16,2048]{3,2,1,0:T(8,128)(2,1)} %get-tuple-element.3), calls=%async_computation | async-start | bytes 4194304 | tf_op jit(solution)/shard_map/all_to_all | solution.py:79
  75.3 0.0 collective-permute-done
  75.3 4.6 %add_convert_fusion.6 = bf16[1,32,16,2048]{3,2,1,0:T(8,128)(2,1)} fusion(bf16[1,32,16,2048]{3,2,1,0:T(8,128)(2,1)} %collective-permute-done, bf16[1,32,16,2048]{3,2,1,0:T(8,128)(2,1)} %param.5, f32[]{:T(128)} %bitcast.2, f32[]{:T(128)} %bitcast.1), kind=kLoop, calls=%fused_computation.14 | loop fusion | flops 6291456 | bytes 6291464 | tf_op jit(solution)/shard_map/convert_element_type | solution.py:28
  79.9 1.0 collective-permute-start.1
  80.9 23.4 %all-to-all-done = bf16[32,1,16,2048]{3,2,1,0:T(8,128)(2,1)S(1)} async-done(((bf16[32,1,16,2048]{3,2,1,0:T(8,128)(2,1)}), bf16[32,1,16,2048]{3,2,1,0:T(8,128)(2,1)S(1)}, u32[]{:S(2)}, u32[]{:S(2)}) %all-to-all-start) | async-done | bytes 2097184 | tf_op jit(solution)/shard_map/all_to_all | solution.py:79
  104.3 1.7 fusion
  106.7 0.4 fusion.1
  107.1 0.0 copy-start.4
  107.1 1.3 copy-done.4
  108.4 1.3 convolution_convert_fusion.4
  109.7 3.8 %add_convert_fusion.4 = bf16[512,2048]{1,0:T(8,128)(2,1)S(1)} fusion(bf16[512,2048]{1,0:T(8,128)(2,1)} %bitcast.46, bf16[512,512]{1,0:T(8,128)(2,1)S(1)} %convolution_convert_fusion.4), kind=kOutput, calls=%fused_computation.10 | convolution fusion | flops 1347682304 | bytes 4718592 | tf_op jit(solution)/shard_map/kmp,kpn->kmn/dot_general | solution.py:56
  113.5 1.3 convolution_convert_fusion.3
  114.8 2.9 %add_convert_fusion.3 = bf16[512,2048]{1,0:T(8,128)(2,1)} fusion(bf16[512,2048]{1,0:T(8,128)(2,1)S(1)} %add_convert_fusion.4, bf16[512,512]{1,0:T(8,128)(2,1)S(1)} %convolution_convert_fusion.3), kind=kOutput, calls=%fused_computation.9 | convolution fusion | flops 1347682304 | bytes 4718592 | tf_op jit(solution)/shard_map/kmp,kpn->kmn/dot_general | solution.py:56
  117.6 0.0 copy-start.6
  117.6 3.6 %convolution_convert_fusion.2 = bf16[512,512]{1,0:T(8,128)(2,1)S(1)} fusion(bf16[512,2048]{1,0:T(8,128)(2,1)} %add_convert_fusion.3), kind=kOutput, calls=%fused_computation.35 | convolution fusion | flops 1074003968 | bytes 2621440 | tf_op jit(solution)/shard_map/kmn,kpn->kmp/dot_general | solution.py:47
  121.3 0.0 copy-done.6
  121.3 2.9 %add_convert_fusion.2 = bf16[512,2048]{1,0:T(8,128)(2,1)} fusion(bf16[512,2048]{1,0:T(8,128)(2,1)S(1)} %copy-done.6, bf16[512,512]{1,0:T(8,128)(2,1)S(1)} %convolution_convert_fusion.2), kind=kOutput, calls=%fused_computation.8 | convolution fusion | flops 1347682304 | bytes 4718592 | tf_op jit(solution)/shard_map/kmp,kpn->kmn/dot_general | solution.py:56
  124.2 0.0 copy-start.7
  124.2 3.6 %convolution_convert_fusion.1 = bf16[512,512]{1,0:T(8,128)(2,1)S(1)} fusion(bf16[512,2048]{1,0:T(8,128)(2,1)} %add_convert_fusion.2), kind=kOutput, calls=%fused_computation.34 | convolution fusion | flops 1074003968 | bytes 2621440 | tf_op jit(solution)/shard_map/kmn,kpn->kmp/dot_general | solution.py:47
  127.8 0.0 copy-done.7
  127.8 2.9 %add_convert_fusion.1 = bf16[512,2048]{1,0:T(8,128)(2,1)} fusion(bf16[512,2048]{1,0:T(8,128)(2,1)S(1)} %copy-done.7, bf16[512,512]{1,0:T(8,128)(2,1)S(1)} %convolution_convert_fusion.1), kind=kOutput, calls=%fused_computation.7 | convolution fusion | flops 1347682304 | bytes 4718592 | tf_op jit(solution)/shard_map/kmp,kpn->kmn/dot_general | solution.py:56
  130.7 3.5 %convolution_convert_fusion = bf16[512,512]{1,0:T(8,128)(2,1)S(1)} fusion(bf16[512,2048]{1,0:T(8,128)(2,1)} %add_convert_fusion.1), kind=kOutput, calls=%fused_computation.33 | convolution fusion | flops 1074003968 | bytes 2621440 | tf_op jit(solution)/shard_map/kmn,kpn->kmp/dot_general | solution.py:47
  134.2 4.1 %fusion.2 = bf16[1,1,512,2048]{3,2,1,0:T(8,128)(2,1)S(1)} fusion(bf16[512,2048]{1,0:T(8,128)(2,1)} %add_convert_fusion.1, bf16[512,512]{1,0:T(8,128)(2,1)S(1)} %convolution_convert_fusion), kind=kOutput, calls=%fused_computation.15 | convolution fusion | flops 1350828032 | bytes 4718592 | tf_op jit(solution)/shard_map/kmp,kpn->kmn/dot_general | solution.py:56
  138.3 5.2 %copy.13 = bf16[1,1,512,2048]{3,1,0,2:T(2,128)(2,1)} copy(bf16[1,1,512,2048]{3,2,1,0:T(8,128)(2,1)S(1)} %fusion.2) | data formatting | bytes 4194304 | tf_op jit(solution)/shard_map/broadcast_in_dim | solution.py:64
  143.5 0.5 broadcast.97
  144.0 13.2 %reduce.2 = bf16[512,2048]{1,0:T(8,128)(2,1)S(1)} reduce(bf16[512,1,1,2048]{3,2,1,0:T(2,128)(2,1)} %bitcast.41, bf16[]{:T(256)} %broadcast.97), dimensions={1,2}, to_apply=%bitcast.40.reduce_sub_computation | reduce | bytes 4194306
  157.2 2.8 %reshape.216 = bf16[32,2,16384]{2,1,0:T(2,128)(2,1)} reshape(bf16[512,2048]{1,0:T(8,128)(2,1)S(1)} %reduce.2) | data formatting | bytes 4194304
  159.9 35.0 %all_to_all.8 = bf16[32,2,16384]{2,1,0:T(2,128)(2,1)S(1)} all-to-all(bf16[32,2,16384]{2,1,0:T(2,128)(2,1)} %reshape.216), channel_id=1, replica_groups=mesh['rep'=4,'shard'=32] {'shard'}, dimensions={0} | all-to-all | bytes 4194304 | tf_op jit(solution)/shard_map/all_to_all | solution.py:65
  195.0 6.7 %reshape.217 = bf16[512,1,1,2048]{3,2,1,0:T(2,128)(2,1)} reshape(bf16[32,2,16384]{2,1,0:T(2,128)(2,1)S(1)} %all_to_all.8) | data formatting | bytes 4194304
  201.7 3.5 %copy.11 = bf16[1,1,512,2048]{3,2,0,1:T(8,128)(2,1)S(1)} copy(bf16[1,1,512,2048]{3,1,0,2:T(2,128)(2,1)} %bitcast.42) | data formatting | bytes 4194304
  205.2 0.0 copy-start.1
  205.2 0.0 collective-permute-done.1
  205.2 5.8 %subtract_convert_fusion = bf16[1,32,16,2048]{3,2,1,0:T(8,128)(2,1)} fusion(bf16[1,32,16,2048]{3,2,1,0:T(8,128)(2,1)S(1)} %bitcast.43, bf16[1,32,16,2048]{3,2,1,0:T(8,128)(2,1)} %collective-permute-done.1, bf16[1,32,16,2048]{3,2,1,0:T(8,128)(2,1)} %add_convert_fusion.6, f32[]{:T(128)} %bitcast.3, f32[]{:T(128)} %bitcast), kind=kLoop, calls=%fused_computation.4 | loop fusion | flops 11534336 | bytes 8388616 | tf_op jit(solution)/shard_map/convert_element_type | solution.py:81
  211.0 0.0 copy-done.1
  (1 shorter events, 0.0 us)
Async XLA Ops:
  0.6 3.8 %copy-start.5 = (s32[4,2]{0,1:T(2,128)S(1)}, s32[4,2]{0,1:T(2,128)}, u32[]{:S(2)}) copy-start(s32[4,2]{0,1:T(2,128)} %param.9) | copy-start | bytes 100
  4.5 4.4 %collective-permute-start.2 = (bf16[1,32,16,2048]{3,2,1,0:T(8,128)(2,1)}, bf16[1,32,16,2048]{3,2,1,0:T(8,128)(2,1)S(1)}, u32[]{:S(2)}, u32[]{:S(2)}) collective-permute-start(bf16[1,32,16,2048]{3,2,1,0:T(8,128)(2,1)} %convert_element_type.215), channel_id=1, source_target_pairs={{0,32},{32,0},{64,96},{96,64},{1,33},{33,1},{65,97},{97,65},{2,34}... | collective-permute-start | bytes 6291464 | tf_op jit(solution)/shard_map/ppermute | solution.py:18
  8.8 51.1 %copy-start = (f32[1,32,16,2048]{3,2,1,0:T(8,128)S(1)}, f32[1,32,16,2048]{3,2,1,0:T(8,128)}, u32[]{:S(2)}) copy-start(f32[1,32,16,2048]{3,2,1,0:T(8,128)} %param.6) | copy-start | bytes 12582916
  8.8 51.1 %copy-start.2 = (bf16[1,32,16,2048]{3,2,1,0:T(8,128)(2,1)S(1)}, bf16[1,32,16,2048]{3,2,1,0:T(8,128)(2,1)}, u32[]{:S(2)}) copy-start(bf16[1,32,16,2048]{3,2,1,0:T(8,128)(2,1)} %param.8) | copy-start | bytes 6291460
  8.8 51.1 %copy-start.3 = (bf16[1,32,16,2048]{3,2,1,0:T(8,128)(2,1)S(1)}, bf16[1,32,16,2048]{3,2,1,0:T(8,128)(2,1)}, u32[]{:S(2)}) copy-start(bf16[1,32,16,2048]{3,2,1,0:T(8,128)(2,1)} %param.7) | copy-start | bytes 6291460
  11.9 48.0 %collective-permute-start.3 = (bf16[1,32,16,2048]{3,2,1,0:T(8,128)(2,1)S(1)}, bf16[1,32,16,2048]{3,2,1,0:T(8,128)(2,1)S(1)}, u32[]{:S(2)}, u32[]{:S(2)}) collective-permute-start(bf16[1,32,16,2048]{3,2,1,0:T(8,128)(2,1)S(1)} %fusion.3), channel_id=1, source_target_pairs={{0,64},{32,96},{64,0},{96,32},{1,65},{33,97},{65,1},{97,33},{2,66}... | collective-permute-start | bytes 6291464 | tf_op jit(solution)/shard_map/ppermute | solution.py:18
  14.0 61.3 %collective-permute-start = (bf16[1,32,16,2048]{3,2,1,0:T(8,128)(2,1)}, bf16[1,32,16,2048]{3,2,1,0:T(8,128)(2,1)}, u32[]{:S(2)}, u32[]{:S(2)}) collective-permute-start(bf16[1,32,16,2048]{3,2,1,0:T(8,128)(2,1)} %param.5), channel_id=1, source_target_pairs={{0,32},{32,0},{64,96},{96,64},{1,33},{33,1},{65,97},{97,65},{2,34}... | collective-permute-start | bytes 6291464 | tf_op jit(solution)/shard_map/ppermute | solution.py:18
  64.9 39.4 %all-to-all-start = ((bf16[32,1,16,2048]{3,2,1,0:T(8,128)(2,1)}), bf16[32,1,16,2048]{3,2,1,0:T(8,128)(2,1)S(1)}, u32[]{:S(2)}, u32[]{:S(2)}) async-start(bf16[32,1,16,2048]{3,2,1,0:T(8,128)(2,1)} %get-tuple-element.3), calls=%async_computation | async-start | bytes 4194304 | tf_op jit(solution)/shard_map/all_to_all | solution.py:79
  79.9 125.3 %collective-permute-start.1 = (bf16[1,32,16,2048]{3,2,1,0:T(8,128)(2,1)}, bf16[1,32,16,2048]{3,2,1,0:T(8,128)(2,1)}, u32[]{:S(2)}, u32[]{:S(2)}) collective-permute-start(bf16[1,32,16,2048]{3,2,1,0:T(8,128)(2,1)} %add_convert_fusion.6), channel_id=1, source_target_pairs={{0,64},{32,96},{64,0},{96,32},{1,65},{33,97},{65,1},{97,33},{2,66}... | collective-permute-start | bytes 6291464 | tf_op jit(solution)/shard_map/ppermute | solution.py:18
  107.1 1.3 copy-start.4
  117.6 3.7 %copy-start.6 = (bf16[512,2048]{1,0:T(8,128)(2,1)S(1)}, bf16[512,2048]{1,0:T(8,128)(2,1)}, u32[]{:S(2)}) copy-start(bf16[512,2048]{1,0:T(8,128)(2,1)} %add_convert_fusion.3) | copy-start | bytes 6291460
  124.2 3.7 %copy-start.7 = (bf16[512,2048]{1,0:T(8,128)(2,1)S(1)}, bf16[512,2048]{1,0:T(8,128)(2,1)}, u32[]{:S(2)}) copy-start(bf16[512,2048]{1,0:T(8,128)(2,1)} %add_convert_fusion.2) | copy-start | bytes 6291460
  205.2 5.8 %copy-start.1 = (bf16[1,1,512,2048]{3,2,0,1:T(8,128)(2,1)}, bf16[1,1,512,2048]{3,2,0,1:T(8,128)(2,1)S(1)}, u32[]{:S(2)}) copy-start(bf16[1,1,512,2048]{3,2,0,1:T(8,128)(2,1)S(1)} %copy.11) | copy-start | bytes 6291460
where the time goes:
time: 211 us
  waiting for transfers between devices  70.5 us (33%)
  other arithmetic  37.4 us (18%)
  blocking collectives  35 us (17%)
  matrix products  29.8 us (14%)
  local copies, waits for them, and re-layouts  20.6 us (10%)
  starting transfers between devices  13.6 us (6%)
  between operations  4.08 us (2%)
    ppermute x4, waiting for transfers between devices, swapped(): lax.ppermute(shard, axis, [(i, i ^ 1 << bit) for i in range(lax.axis_size...  47.1 us
    all_to_all x1, blocking collectives, settle(): lax.all_to_all(update_block, 'shard', split_axis=2, concat_axis=0, tiled=...  35 us
    all_to_all x1, waiting for transfers between devices, local(): lax.all_to_all(packed, 'shard', split_axis=0, concat_axis=2, tiled=True)  23.4 us
    dot_general x5, matrix products, orthogonalize(): jnp.einsum('kmp,kpn->kmn', polynomial, iterate, preferred_element_type=jn...  16.5 us
    unnamed x20, local copies, waits for them, and re-layouts  14.8 us
    dot_general x5, matrix products, orthogonalize(): jnp.einsum('kmn,kpn->kmp', iterate, iterate, preferred_element_type=jnp.f...  13.4 us
    unnamed x1, other arithmetic  13.2 us
    all_to_all x1, starting transfers between devices, local(): lax.all_to_all(packed, 'shard', split_axis=0, concat_axis=2, tiled=True)  10.5 us
  transfers between devices with their start and end apart: 5, of which 3 were waited for; matrix products, arithmetic and copies ran while one was open for 35% of the time, Pallas kernels for 0%

commit v1 on v0

--- a/solution.py
+++ b/solution.py
@@ -62,7 +62,10 @@
 
 def settle(block_in):
     update_block = orthogonalize(block_in[0])[None]
-    return lax.all_to_all(update_block, "shard", split_axis=2, concat_axis=0, tiled=True)
+    shards = lax.axis_size("shard")
+    rows = update_block.shape[2] // shards
+    cut = update_block.reshape(shards, update_block.shape[1], rows, update_block.shape[3])
+    return lax.all_to_all(cut, "shard", split_axis=0, concat_axis=0, tiled=True)
 
 
 def local(weight, tracker, grad_new, grad_old, mix_keep):

time: 211 us -> 180 us (0.85)
  local copies, waits for them, and re-layouts: 20.6 us -> 3.25 us
  other arithmetic: 37.4 us -> 23.5 us
    unnamed x1 -> x0, other arithmetic: 13.2 us -> none
    unnamed x20 -> x15, local copies, waits for them, and re-layouts: 14.8 us -> 2.65 us
    broadcast_in_dim x1 -> x0, local copies, waits for them, and re-layouts: 5.18 us -> none  [settle(): update_block = orthogonalize(block_in[0])[None]]
  transfers between devices with their start and end apart: 5 -> 5, of which waited for: 3 -> 3; matrix products, arithmetic and copies ran while one was open for 35% -> 23% of each run, Pallas kernels for 0% -> 0%
where the time goes in v1:
time: 180 us
  waiting for transfers between devices  70.5 us (39%)
  blocking collectives  34.9 us (19%)
  matrix products  29.8 us (17%)
  other arithmetic  23.5 us (13%)
  starting transfers between devices  13.6 us (8%)
  between operations  4.05 us (2%)
  local copies, waits for them, and re-layouts  3.25 us (2%)
    ppermute x4, waiting for transfers between devices, swapped(): lax.ppermute(shard, axis, [(i, i ^ 1 << bit) for i in range(lax.axis_size...  47.1 us
    all_to_all x1, blocking collectives, settle(): return lax.all_to_all(cut, 'shard', split_axis=0, concat_axis=0, tiled=True)  34.9 us
    all_to_all x1, waiting for transfers between devices, local(): lax.all_to_all(packed, 'shard', split_axis=0, concat_axis=2, tiled=True)  23.4 us
    dot_general x5, matrix products, orthogonalize(): jnp.einsum('kmp,kpn->kmn', polynomial, iterate, preferred_element_type=jn...  16.5 us
    dot_general x5, matrix products, orthogonalize(): jnp.einsum('kmn,kpn->kmp', iterate, iterate, preferred_element_type=jnp.f...  13.4 us
    all_to_all x1, starting transfers between devices, local(): lax.all_to_all(packed, 'shard', split_axis=0, concat_axis=2, tiled=True)  10.5 us
    convert_element_type x2, other arithmetic, gossip_tracker(): values.astype(jnp.bfloat16)  6.91 us
    convert_element_type x1, other arithmetic, local(): (mixed_w.astype(jnp.float32) - learn_rate * update.astype(jnp.float32)).a...  5.04 us
  transfers between devices with their start and end apart: 5, of which 3 were waited for; matrix products, arithmetic and copies ran while one was open for 23% of the time, Pallas kernels for 0%

profile of v1, /device:TPU:0, one launch (start us, length us, event | category | flops | bytes accessed | tf_op | source)
XLA Modules:
  0.0 179.5 jit_solution(1223221493856264984)
XLA Ops:
  0.6 0.0 copy-start.4
  0.6 3.8 %convert_element_type.215 = bf16[1,32,16,2048]{3,2,1,0:T(8,128)(2,1)} convert(f32[1,32,16,2048]{3,2,1,0:T(8,128)} %param.6) | non-fusion elementwise | flops 1048576 | bytes 6291456 | tf_op jit(solution)/shard_map/convert_element_type | solution.py:34
  4.5 0.0 collective-permute-start.2
  4.5 0.0 copy-done.4
  4.5 0.1 constant_dynamic-slice_fusion
  4.6 0.5 fusion.33
  6.4 2.5 %collective-permute-done.2 = bf16[1,32,16,2048]{3,2,1,0:T(8,128)(2,1)S(1)} collective-permute-done((bf16[1,32,16,2048]{3,2,1,0:T(8,128)(2,1)}, bf16[1,32,16,2048]{3,2,1,0:T(8,128)(2,1)S(1)}, u32[]{:S(2)}, u32[]{:S(2)}) %collective-permute-start.2) | collective-permute-done | bytes 2097184 | tf_op jit(solution)/shard_map/ppermute | solution.py:18
  8.8 0.0 copy-start
  8.8 0.0 copy-start.1
  8.8 0.0 copy-start.2
  8.8 3.1 %fusion.2 = bf16[1,32,16,2048]{3,2,1,0:T(8,128)(2,1)S(1)} fusion(bf16[1,32,16,2048]{3,2,1,0:T(8,128)(2,1)S(1)} %collective-permute-done.2, f32[1,32,16,2048]{3,2,1,0:T(8,128)} %param.6, f32[]{:T(128)} %bitcast.2, f32[]{:T(128)} %bitcast.1), kind=kLoop, calls=%fused_computation.15 | loop fusion | flops 5242880 | bytes 8388616 | tf_op jit(solution)/shard_map/convert_element_type | solution.py:34
  11.9 2.1 %collective-permute-start.3 = (bf16[1,32,16,2048]{3,2,1,0:T(8,128)(2,1)S(1)}, bf16[1,32,16,2048]{3,2,1,0:T(8,128)(2,1)S(1)}, u32[]{:S(2)}, u32[]{:S(2)}) collective-permute-start(bf16[1,32,16,2048]{3,2,1,0:T(8,128)(2,1)S(1)} %fusion.2), channel_id=1, source_target_pairs={{0,64},{32,96},{64,0},{96,32},{1,65},{33,97},{65,1},{97,33},{2,66}... | collective-permute-start | bytes 6291464 | tf_op jit(solution)/shard_map/ppermute | solution.py:18
  14.0 0.0 collective-permute-start
  15.3 44.6 %collective-permute-done.3 = bf16[1,32,16,2048]{3,2,1,0:T(8,128)(2,1)S(1)} collective-permute-done((bf16[1,32,16,2048]{3,2,1,0:T(8,128)(2,1)S(1)}, bf16[1,32,16,2048]{3,2,1,0:T(8,128)(2,1)S(1)}, u32[]{:S(2)}, u32[]{:S(2)}) %collective-permute-start.3) | collective-permute-done | bytes 2097184 | tf_op jit(solution)/shard_map/ppermute | solution.py:18
  60.0 0.0 copy-done
  60.0 0.0 copy-done.1
  60.0 0.0 copy-done.2
  60.0 4.9 %convert_bitcast_fusion = (bf16[32,1,16,2048]{3,2,1,0:T(8,128)(2,1)}, f32[1,32,16,2048]{3,2,1,0:T(8,128)}) fusion(bf16[1,32,16,2048]{3,2,1,0:T(8,128)(2,1)S(1)} %copy-done.1, bf16[1,32,16,2048]{3,2,1,0:T(8,128)(2,1)S(1)} %copy-done.2, bf16[1,32,16,2048]{3,2,1,0:T(8,128)(2,1)S(1)} %collective-permute-done.3, f32[]{:T(128)} %bitcast.3, ...), kind=kLoop, calls=%fused_computation.16 | loop fusion | flops 13631488 | bytes 18874384 | tf_op jit(solution)/shard_map/reshape | solution.py:81
  64.9 10.5 %all-to-all-start = ((bf16[32,1,16,2048]{3,2,1,0:T(8,128)(2,1)}), bf16[32,1,16,2048]{3,2,1,0:T(8,128)(2,1)S(1)}, u32[]{:S(2)}, u32[]{:S(2)}) async-start(bf16[32,1,16,2048]{3,2,1,0:T(8,128)(2,1)} %get-tuple-element.3), calls=%async_computation | async-start | bytes 4194304 | tf_op jit(solution)/shard_map/all_to_all | solution.py:82
  75.3 0.0 collective-permute-done
  75.3 4.6 %add_convert_fusion.6 = bf16[1,32,16,2048]{3,2,1,0:T(8,128)(2,1)} fusion(bf16[1,32,16,2048]{3,2,1,0:T(8,128)(2,1)} %collective-permute-done, bf16[1,32,16,2048]{3,2,1,0:T(8,128)(2,1)} %param.5, f32[]{:T(128)} %bitcast.2, f32[]{:T(128)} %bitcast.1), kind=kLoop, calls=%fused_computation.14 | loop fusion | flops 6291456 | bytes 6291464 | tf_op jit(solution)/shard_map/convert_element_type | solution.py:28
  79.9 1.0 collective-permute-start.1
  80.9 23.4 %all-to-all-done = bf16[32,1,16,2048]{3,2,1,0:T(8,128)(2,1)S(1)} async-done(((bf16[32,1,16,2048]{3,2,1,0:T(8,128)(2,1)}), bf16[32,1,16,2048]{3,2,1,0:T(8,128)(2,1)S(1)}, u32[]{:S(2)}, u32[]{:S(2)}) %all-to-all-start) | async-done | bytes 2097184 | tf_op jit(solution)/shard_map/all_to_all | solution.py:82
  104.3 1.7 fusion
  106.7 0.4 fusion.1
  107.1 0.0 copy-start.3
  107.1 1.3 copy-done.3
  108.4 1.3 convolution_convert_fusion.4
  109.7 3.8 %add_convert_fusion.4 = bf16[512,2048]{1,0:T(8,128)(2,1)S(1)} fusion(bf16[512,2048]{1,0:T(8,128)(2,1)} %bitcast.39, bf16[512,512]{1,0:T(8,128)(2,1)S(1)} %convolution_convert_fusion.4), kind=kOutput, calls=%fused_computation.10 | convolution fusion | flops 1347682304 | bytes 4718592 | tf_op jit(solution)/shard_map/kmp,kpn->kmn/dot_general | solution.py:56
  113.5 1.3 convolution_convert_fusion.3
  114.8 2.9 %add_convert_fusion.3 = bf16[512,2048]{1,0:T(8,128)(2,1)} fusion(bf16[512,2048]{1,0:T(8,128)(2,1)S(1)} %add_convert_fusion.4, bf16[512,512]{1,0:T(8,128)(2,1)S(1)} %convolution_convert_fusion.3), kind=kOutput, calls=%fused_computation.9 | convolution fusion | flops 1347682304 | bytes 4718592 | tf_op jit(solution)/shard_map/kmp,kpn->kmn/dot_general | solution.py:56
  117.6 0.0 copy-start.5
  117.6 3.6 %convolution_convert_fusion.2 = bf16[512,512]{1,0:T(8,128)(2,1)S(1)} fusion(bf16[512,2048]{1,0:T(8,128)(2,1)} %add_convert_fusion.3), kind=kOutput, calls=%fused_computation.34 | convolution fusion | flops 1074003968 | bytes 2621440 | tf_op jit(solution)/shard_map/kmn,kpn->kmp/dot_general | solution.py:47
  121.3 0.0 copy-done.5
  121.3 2.9 %add_convert_fusion.2 = bf16[512,2048]{1,0:T(8,128)(2,1)} fusion(bf16[512,2048]{1,0:T(8,128)(2,1)S(1)} %copy-done.5, bf16[512,512]{1,0:T(8,128)(2,1)S(1)} %convolution_convert_fusion.2), kind=kOutput, calls=%fused_computation.8 | convolution fusion | flops 1347682304 | bytes 4718592 | tf_op jit(solution)/shard_map/kmp,kpn->kmn/dot_general | solution.py:56
  124.2 0.0 copy-start.6
  124.2 3.6 %convolution_convert_fusion.1 = bf16[512,512]{1,0:T(8,128)(2,1)S(1)} fusion(bf16[512,2048]{1,0:T(8,128)(2,1)} %add_convert_fusion.2), kind=kOutput, calls=%fused_computation.33 | convolution fusion | flops 1074003968 | bytes 2621440 | tf_op jit(solution)/shard_map/kmn,kpn->kmp/dot_general | solution.py:47
  127.8 0.0 copy-done.6
  127.8 2.9 %add_convert_fusion.1 = bf16[512,2048]{1,0:T(8,128)(2,1)} fusion(bf16[512,2048]{1,0:T(8,128)(2,1)S(1)} %copy-done.6, bf16[512,512]{1,0:T(8,128)(2,1)S(1)} %convolution_convert_fusion.1), kind=kOutput, calls=%fused_computation.7 | convolution fusion | flops 1347682304 | bytes 4718592 | tf_op jit(solution)/shard_map/kmp,kpn->kmn/dot_general | solution.py:56
  130.7 3.5 %convolution_convert_fusion = bf16[512,512]{1,0:T(8,128)(2,1)S(1)} fusion(bf16[512,2048]{1,0:T(8,128)(2,1)} %add_convert_fusion.1), kind=kOutput, calls=%fused_computation.32 | convolution fusion | flops 1074003968 | bytes 2621440 | tf_op jit(solution)/shard_map/kmn,kpn->kmp/dot_general | solution.py:47
  134.2 4.1 %multiply_convert_fusion = bf16[512,2048]{1,0:T(8,128)(2,1)S(1)} fusion(bf16[512,2048]{1,0:T(8,128)(2,1)} %add_convert_fusion.1, bf16[512,512]{1,0:T(8,128)(2,1)S(1)} %convolution_convert_fusion), kind=kOutput, calls=%fused_computation.5 | convolution fusion | flops 1350828032 | bytes 4718592 | tf_op jit(solution)/shard_map/kmp,kpn->kmn/dot_general | solution.py:56
  138.3 34.9 %all_to_all.14 = bf16[32,1,16,2048]{3,2,1,0:T(8,128)(2,1)S(1)} all-to-all(bf16[32,1,16,2048]{3,2,1,0:T(8,128)(2,1)S(1)} %bitcast.40), channel_id=1, replica_groups=mesh['rep'=4,'shard'=32] {'shard'}, dimensions={0} | all-to-all | bytes 4194304 | tf_op jit(solution)/shard_map/all_to_all | solution.py:68
  173.2 0.0 collective-permute-done.1
  173.2 5.0 %subtract_convert_fusion = bf16[1,32,16,2048]{3,2,1,0:T(8,128)(2,1)} fusion(bf16[1,32,16,2048]{3,2,1,0:T(8,128)(2,1)} %collective-permute-done.1, bf16[1,32,16,2048]{3,2,1,0:T(8,128)(2,1)} %add_convert_fusion.6, f32[]{:T(128)} %bitcast.3, f32[]{:T(128)} %bitcast, bf16[32,1,16,2048]{3,2,1,0:T(8,128)(2,1)S(1)} %all_to_all.14), kind=kLoop, calls=%fused_computation.4 | loop fusion | flops 11534336 | bytes 8388616 | tf_op jit(solution)/shard_map/convert_element_type | solution.py:84
  178.2 1.3 copy.10
  (1 shorter events, 0.0 us)
Async XLA Ops:
  0.6 3.8 %copy-start.4 = (s32[4,2]{0,1:T(2,128)S(1)}, s32[4,2]{0,1:T(2,128)}, u32[]{:S(2)}) copy-start(s32[4,2]{0,1:T(2,128)} %param.9) | copy-start | bytes 100
  4.5 4.4 %collective-permute-start.2 = (bf16[1,32,16,2048]{3,2,1,0:T(8,128)(2,1)}, bf16[1,32,16,2048]{3,2,1,0:T(8,128)(2,1)S(1)}, u32[]{:S(2)}, u32[]{:S(2)}) collective-permute-start(bf16[1,32,16,2048]{3,2,1,0:T(8,128)(2,1)} %convert_element_type.215), channel_id=1, source_target_pairs={{0,32},{32,0},{64,96},{96,64},{1,33},{33,1},{65,97},{97,65},{2,34}... | collective-permute-start | bytes 6291464 | tf_op jit(solution)/shard_map/ppermute | solution.py:18
  8.8 51.1 %copy-start = (f32[1,32,16,2048]{3,2,1,0:T(8,128)S(1)}, f32[1,32,16,2048]{3,2,1,0:T(8,128)}, u32[]{:S(2)}) copy-start(f32[1,32,16,2048]{3,2,1,0:T(8,128)} %param.6) | copy-start | bytes 12582916
  8.8 51.1 %copy-start.1 = (bf16[1,32,16,2048]{3,2,1,0:T(8,128)(2,1)S(1)}, bf16[1,32,16,2048]{3,2,1,0:T(8,128)(2,1)}, u32[]{:S(2)}) copy-start(bf16[1,32,16,2048]{3,2,1,0:T(8,128)(2,1)} %param.8) | copy-start | bytes 6291460
  8.8 51.1 %copy-start.2 = (bf16[1,32,16,2048]{3,2,1,0:T(8,128)(2,1)S(1)}, bf16[1,32,16,2048]{3,2,1,0:T(8,128)(2,1)}, u32[]{:S(2)}) copy-start(bf16[1,32,16,2048]{3,2,1,0:T(8,128)(2,1)} %param.7) | copy-start | bytes 6291460
  11.9 48.0 %collective-permute-start.3 = (bf16[1,32,16,2048]{3,2,1,0:T(8,128)(2,1)S(1)}, bf16[1,32,16,2048]{3,2,1,0:T(8,128)(2,1)S(1)}, u32[]{:S(2)}, u32[]{:S(2)}) collective-permute-start(bf16[1,32,16,2048]{3,2,1,0:T(8,128)(2,1)S(1)} %fusion.2), channel_id=1, source_target_pairs={{0,64},{32,96},{64,0},{96,32},{1,65},{33,97},{65,1},{97,33},{2,66}... | collective-permute-start | bytes 6291464 | tf_op jit(solution)/shard_map/ppermute | solution.py:18
  14.0 61.3 %collective-permute-start = (bf16[1,32,16,2048]{3,2,1,0:T(8,128)(2,1)}, bf16[1,32,16,2048]{3,2,1,0:T(8,128)(2,1)}, u32[]{:S(2)}, u32[]{:S(2)}) collective-permute-start(bf16[1,32,16,2048]{3,2,1,0:T(8,128)(2,1)} %param.5), channel_id=1, source_target_pairs={{0,32},{32,0},{64,96},{96,64},{1,33},{33,1},{65,97},{97,65},{2,34}... | collective-permute-start | bytes 6291464 | tf_op jit(solution)/shard_map/ppermute | solution.py:18
  64.9 39.4 %all-to-all-start = ((bf16[32,1,16,2048]{3,2,1,0:T(8,128)(2,1)}), bf16[32,1,16,2048]{3,2,1,0:T(8,128)(2,1)S(1)}, u32[]{:S(2)}, u32[]{:S(2)}) async-start(bf16[32,1,16,2048]{3,2,1,0:T(8,128)(2,1)} %get-tuple-element.3), calls=%async_computation | async-start | bytes 4194304 | tf_op jit(solution)/shard_map/all_to_all | solution.py:82
  79.9 93.3 %collective-permute-start.1 = (bf16[1,32,16,2048]{3,2,1,0:T(8,128)(2,1)}, bf16[1,32,16,2048]{3,2,1,0:T(8,128)(2,1)}, u32[]{:S(2)}, u32[]{:S(2)}) collective-permute-start(bf16[1,32,16,2048]{3,2,1,0:T(8,128)(2,1)} %add_convert_fusion.6), channel_id=1, source_target_pairs={{0,64},{32,96},{64,0},{96,32},{1,65},{33,97},{65,1},{97,33},{2,66}... | collective-permute-start | bytes 6291464 | tf_op jit(solution)/shard_map/ppermute | solution.py:18
  107.1 1.3 copy-start.3
  117.6 3.7 %copy-start.5 = (bf16[512,2048]{1,0:T(8,128)(2,1)S(1)}, bf16[512,2048]{1,0:T(8,128)(2,1)}, u32[]{:S(2)}) copy-start(bf16[512,2048]{1,0:T(8,128)(2,1)} %add_convert_fusion.3) | copy-start | bytes 6291460
  124.2 3.7 %copy-start.6 = (bf16[512,2048]{1,0:T(8,128)(2,1)S(1)}, bf16[512,2048]{1,0:T(8,128)(2,1)}, u32[]{:S(2)}) copy-start(bf16[512,2048]{1,0:T(8,128)(2,1)} %add_convert_fusion.2) | copy-start | bytes 6291460

commit v2 on v0

v2 whole, which is shorter than its diff:
```python
import functools
import math

import jax
import jax.numpy as jnp
from jax import lax
from jax.experimental import pallas as pl
from jax.experimental.pallas import tpu as pltpu
from jax.sharding import PartitionSpec as P

MESH = pl.DeviceIdType.MESH
NS_STEPS = 5

coeff_a = 3.4445
coeff_b = -4.775
coeff_c = 2.0315
learn_rate = 0.05

X_SIZE, Z_SIZE = 4, 2
STRIDE = 13
LAG = 8


def peer_at(me, step, shards):
    y_size = shards // (X_SIZE * Z_SIZE)
    offset = lax.rem(step * STRIDE, shards)
    x = lax.rem(lax.rem(me, X_SIZE) + lax.rem(offset, X_SIZE), X_SIZE)
    z = lax.rem(lax.rem(lax.div(me, X_SIZE), Z_SIZE) + lax.rem(lax.div(offset, X_SIZE), Z_SIZE), Z_SIZE)
    y = lax.rem(lax.div(me, X_SIZE * Z_SIZE) + lax.div(offset, X_SIZE * Z_SIZE), y_size)
    return (y * Z_SIZE + z) * X_SIZE + x


def greet(rep, me, shards, others):
    barrier = pltpu.get_barrier_semaphore()

    @pl.loop(1, shards)
    def _(step):
        pl.semaphore_signal(barrier, inc=1, device_id=(rep, peer_at(me, step, shards)), device_id_type=MESH)

    for other in others:
        pl.semaphore_signal(barrier, inc=1, device_id=(other, me), device_id_type=MESH)
    return lambda: pl.semaphore_wait(barrier, shards - 1 + len(others))


def shares(keep, rep, bit):
    own = keep[rep, bit].astype(jnp.float32) / 16.0
    return own, 1.0 - own


def gossip_kernel(
    shards, keep, y, gn, go, w, x_out, nt, w1_out,
    yv, yb, yp, ub, up, gnv, gov, gs, wv, wp, w1v,
    y_sem, yb_send, yb_recv, u_send, u_recv, g_send, g_recv, nt_sem, in_sem, w_send, w_recv,
):
    rep, me = lax.axis_index("rep"), lax.axis_index("shard")
    core = rep + 1 - 2 * lax.rem(rep, 2)
    side = lax.rem(rep + 2, 4)
    enter = greet(rep, me, shards, (core, side))
    at = lambda step: peer_at(me, step, shards)

    def load_y(step):
        return pltpu.make_async_copy(y.at[at(step)], yv.at[at(step)], y_sem.at[step])

    def send_y(step):
        e = at(step)
        return pltpu.make_async_remote_copy(
            yb.at[e], yp.at[e], yb_send.at[step], yb_recv.at[step], device_id=(core, me), device_id_type=MESH
        )

    def send_u(step):
        e = at(step)
        return pltpu.make_async_remote_copy(
            ub.at[e], up.at[e], u_send.at[step], u_recv.at[step], device_id=(side, me), device_id_type=MESH
        )

    def send_g(step):
        e = at(step)
        return pltpu.make_async_remote_copy(
            gs.at[e], x_out.at[me], g_send.at[step], g_recv.at[step], device_id=(rep, e), device_id_type=MESH
        )

    def store_nt(step):
        e = at(step)
        return pltpu.make_async_copy(yv.at[e], nt.at[e], nt_sem.at[step])

    own_block = pltpu.make_async_copy(gs.at[me], x_out.at[me], g_recv.at[0])
    load_gn = pltpu.make_async_copy(gn, gnv, in_sem.at[0])
    load_go = pltpu.make_async_copy(go, gov, in_sem.at[1])
    load_w = pltpu.make_async_copy(w, wv, in_sem.at[2])
    store_w1 = pltpu.make_async_copy(w1v, w1_out, in_sem.at[3])
    send_w = pltpu.make_async_remote_copy(wv, wp, w_send, w_recv, device_id=(core, me), device_id_type=MESH)

    @pl.loop(0, shards)
    def _(step):
        load_y(step).start()

    load_gn.start()
    load_go.start()
    load_w.start()
    own0, other0 = shares(keep, rep, 0)
    own1, other1 = shares(keep, rep, 1)
    enter()

    @pl.loop(0, shards + LAG + 1)
    def _(tick):
        @pl.when(tick < shards)
        def _():
            load_y(tick).wait()
            e = at(tick)
            yb[e] = yv[e].astype(jnp.bfloat16)

        @pl.when((tick >= 1) & (tick <= shards))
        def _():
            send_y(tick - 1).start()

        @pl.when((tick >= LAG) & (tick < shards + LAG))
        def _():
            send_y(tick - LAG).wait_recv()
            e = at(tick - LAG)
            mixed = own0 * yv[e] + other0 * yp[e].astype(jnp.float32)
            yv[e] = mixed
            ub[e] = mixed.astype(jnp.bfloat16)

        @pl.when(tick >= LAG + 1)
        def _():
            send_u(tick - LAG - 1).start()

    load_w.wait()
    send_w.start()
    load_gn.wait()
    load_go.wait()

    @pl.loop(0, shards + 1)
    def _(tick):
        @pl.when(tick < shards)
        def _():
            send_u(tick).wait_recv()
            e = at(tick)
            fresh = (
                own1 * yv[e] + other1 * up[e].astype(jnp.float32)
                + gnv[e].astype(jnp.float32) - gov[e].astype(jnp.float32)
            )
            yv[e] = fresh
            gs[e] = fresh.astype(jnp.bfloat16)

        @pl.when(tick >= 2)
        def _():
            send_g(tick - 1).start()

        @pl.when(tick == 1)
        def _():
            own_block.start()

        @pl.when(tick >= 1)
        def _():
            store_nt(tick - 1).start()

    send_w.wait()

    @pl.loop(0, shards)
    def _(e):
        w1v[e] = (own0 * wv[e].astype(jnp.float32) + other0 * wp[e].astype(jnp.float32)).astype(jnp.bfloat16)

    store_w1.start()
    own_block.wait()

    @pl.loop(0, shards)
    def _(step):
        send_y(step).wait_send()
        send_u(step).wait_send()
        store_nt(step).wait()

    store_w1.wait()

    @pl.loop(1, shards)
    def _(step):
        send_g(step).wait()


def return_kernel(shards, us, ur, own, send, recv, sem):
    rep, me = lax.axis_index("rep"), lax.axis_index("shard")
    enter = greet(rep, me, shards, ())
    fetch = pltpu.make_async_copy(us.at[me], own, sem.at[0])
    put = pltpu.make_async_copy(own, ur.at[me], sem.at[1])
    fetch.start()

    def send_block(step):
        e = peer_at(me, step, shards)
        return pltpu.make_async_remote_copy(
            us.at[e], ur.at[me], send.at[step], recv.at[step], device_id=(rep, e), device_id_type=MESH
        )

    enter()

    @pl.loop(1, shards)
    def _(step):
        send_block(step).start()

    fetch.wait()
    put.start()
    put.wait()

    @pl.loop(1, shards)
    def _(step):
        send_block(step).wait()


def finish_kernel(keep, w1, w1p, ur, new_weight, update):
    own1, other1 = shares(keep, lax.axis_index("rep"), 1)
    mixed = (own1 * w1[...].astype(jnp.float32) + other1 * w1p[...].astype(jnp.float32)).astype(jnp.bfloat16)
    new_weight[...] = (mixed.astype(jnp.float32) - learn_rate * ur[...].astype(jnp.float32)).astype(jnp.bfloat16)
    update[...] = ur[...]


def orthogonalize(block_in):
    update_scale = 0.2 * math.sqrt(max(block_in.shape[0], block_in.shape[1]))
    values = block_in.astype(jnp.float32)
    frob_norm = jnp.sqrt(jnp.sum(values * values))
    iterate = (values / (frob_norm + 1e-07)).astype(jnp.bfloat16)
    for iteration in range(NS_STEPS):
        gram_matrix = jnp.einsum("mn,pn->mp", iterate, iterate, preferred_element_type=jnp.float32).astype(jnp.bfloat16)
        square = jnp.einsum("mp,pq->mq", gram_matrix, gram_matrix, preferred_element_type=jnp.float32)
        polynomial = (coeff_b * gram_matrix.astype(jnp.float32) + coeff_c * square).astype(jnp.bfloat16)
        product = jnp.einsum("mp,pn->mn", polynomial, iterate, preferred_element_type=jnp.float32)
        iterate = (coeff_a * iterate.astype(jnp.float32) + product).astype(jnp.bfloat16)
    return (update_scale * iterate.astype(jnp.float32)).astype(jnp.bfloat16)


def local(weight, tracker, grad_new, grad_old, mix_keep):
    shards = lax.axis_size("shard")
    block = weight.shape[1:]
    experts, rows, columns = block
    half = jax.ShapeDtypeStruct(block, jnp.bfloat16)
    full = jax.ShapeDtypeStruct(block, jnp.float32)
    anywhere = pl.BlockSpec(memory_space=pl.ANY)
    scalars = pl.BlockSpec(memory_space=pltpu.SMEM)
    vmem_half = pltpu.VMEM(block, jnp.bfloat16)
    dma = pltpu.SemaphoreType.DMA

    x, new_tracker, w1 = pl.pallas_call(
        functools.partial(gossip_kernel, shards),
        out_shape=(half, full, half),
        in_specs=[scalars] + [anywhere] * 4,
        out_specs=(anywhere,) * 3,
        scratch_shapes=[pltpu.VMEM(block, jnp.float32)] + [vmem_half] * 10
        + [dma((shards,))] * 8 + [dma((4,)), dma, dma],
        compiler_params=pltpu.CompilerParams(collective_id=0, has_side_effects=True, vmem_limit_bytes=48 << 20),
        name="gossip",
    )(mix_keep, tracker[0], grad_new[0], grad_old[0], weight[0])

    w1p = lax.ppermute(w1, "rep", [(i, i ^ 2) for i in range(lax.axis_size("rep"))])
    cut = orthogonalize(x.reshape(shards * rows, columns)).reshape(block)

    returned = pl.pallas_call(
        functools.partial(return_kernel, shards),
        out_shape=half,
        in_specs=[anywhere],
        out_specs=anywhere,
        scratch_shapes=[pltpu.VMEM((rows, columns), jnp.bfloat16), dma((shards,)), dma((shards,)), dma((2,))],
        compiler_params=pltpu.CompilerParams(collective_id=1, has_side_effects=True, vmem_limit_bytes=48 << 20),
        cost_estimate=pl.CostEstimate(flops=0, bytes_accessed=100 << 20, transcendentals=0),
        name="giveback",
    )(cut)

    step = 4
    tile = pl.BlockSpec((step, rows, columns), lambda i: (i, 0, 0))
    new_weight, update = pl.pallas_call(
        finish_kernel,
        grid=(experts // step,),
        out_shape=(half, half),
        in_specs=[scalars] + [tile] * 3,
        out_specs=(tile, tile),
        name="finish",
    )(mix_keep, w1, w1p, returned)
    return (new_weight[None], new_tracker[None], update[None])


def solution(mesh):
    spec = P("rep", None, "shard", None)
    return jax.shard_map(
        local,
        mesh=mesh,
        in_specs=(spec, spec, spec, spec, P()),
        out_specs=(spec, spec, spec),
        check_vma=False,
    )
```

time: 211 us -> 172 us (0.82)
  Pallas kernels: 0 us -> 130 us
  waiting for transfers between devices: 70.5 us -> 0.01 us
  other arithmetic: 37.4 us -> 2.08 us
  blocking collectives: 35 us -> 0 us
  starting transfers between devices: 13.6 us -> 1.09 us
  local copies, waits for them, and re-layouts: 20.6 us -> 8.1 us
  between operations: 4.08 us -> 1.44 us
    pallas_call x0 -> x3, Pallas kernels: none -> 130 us  [the longest x1 85.7 us: local(): pl.pallas_call(functools.partial(gossip_kernel, shards), out_shape=(half,...]
    ppermute x4 -> x1, waiting for transfers between devices: 47.1 us -> 0.01 us  [local(): lax.ppermute(w1, 'rep', [(i, i ^ 2) for i in range(lax.axis_size('rep'))])]
    all_to_all x1 -> x0, blocking collectives: 35 us -> none  [settle(): lax.all_to_all(update_block, 'shard', split_axis=2, concat_axis=0, tiled=...]
    all_to_all x1 -> x0, waiting for transfers between devices: 23.4 us -> none  [local(): lax.all_to_all(packed, 'shard', split_axis=0, concat_axis=2, tiled=True)]
    convert_element_type x5 -> x0, other arithmetic: 17.3 us -> none  [the longest x2 6.91 us: gossip_tracker(): values.astype(jnp.bfloat16)]
    unnamed x1 -> x0, other arithmetic: 13.2 us -> none
    all_to_all x1 -> x0, starting transfers between devices: 10.5 us -> none  [local(): lax.all_to_all(packed, 'shard', split_axis=0, concat_axis=2, tiled=True)]
    unnamed x20 -> x12, local copies, waits for them, and re-layouts: 14.8 us -> 8.1 us
  transfers between devices with their start and end apart: 5 -> 1, of which waited for: 3 -> 0; matrix products, arithmetic and copies ran while one was open for 35% -> 18% of each run, Pallas kernels for 0% -> 21%
where the time goes in v2:
time: 172 us
  Pallas kernels  130 us (76%)
  matrix products  29.6 us (17%)
  local copies, waits for them, and re-layouts  8.1 us (5%)
  other arithmetic  2.08 us (1%)
    pallas_call x1, Pallas kernels, local(): pl.pallas_call(functools.partial(gossip_kernel, shards), out_shape=(half,...  85.7 us
    pallas_call x1, Pallas kernels, local(): pl.pallas_call(functools.partial(return_kernel, shards), out_shape=half,...  36.6 us
    dot_general x5, matrix products, orthogonalize(): jnp.einsum('mp,pn->mn', polynomial, iterate, preferred_element_type=jnp.f...  16.2 us
    dot_general x5, matrix products, orthogonalize(): jnp.einsum('mn,pn->mp', iterate, iterate, preferred_element_type=jnp.floa...  13.4 us
    unnamed x12, local copies, waits for them, and re-layouts  8.1 us
    pallas_call x1, Pallas kernels, local(): pl.pallas_call(finish_kernel, grid=(experts // step,), out_shape=(half, h...  7.26 us
  transfers between devices with their start and end apart: 1, of which 0 were waited for; matrix products, arithmetic and copies ran while one was open for 18% of the time, Pallas kernels for 21%

profile of v2, /device:TPU:0, one launch (start us, length us, event | category | flops | bytes accessed | tf_op | source)
XLA Modules:
  0.0 171.8 jit_solution(14904938302672632885)
XLA Ops:
  0.6 0.8 copy.9.keep
  1.4 0.0 copy-start.1
  1.4 85.7 %gossip.1 = (bf16[32,16,2048]{2,1,0:T(8,128)(2,1)S(1)}, f32[32,16,2048]{2,1,0:T(8,128)}, bf16[32,16,2048]{2,1,0:T(8,128)(2,1)}) custom-call(s32[4,2]{1,0:T(4,128)S(1)} %copy.9.keep, f32[32,16,2048]{2,1,0:T(8,128)} %bitcast.35, bf16[32,16,2048]{2,1,0:T(8,128)(2,1)} %bitcast.39, bf16[32,16,2048]{2,1,0:T(8,128)(2,1)} %bitcast.40, bf16[32,16,2048]{2,1,0:T(8,128)(2,1)} %bitcast.41), custom_call_target="tpu_custom_call" | custom-call | tf_op jit(solution)/shard_map/gossip/pallas_call | solution.py:240
  87.1 0.0 copy-done.1
  87.2 1.1 collective-permute-start
  88.2 1.7 fusion
  90.6 0.4 fusion.1
  91.0 0.0 copy-start.2
  91.0 1.3 copy-done.2
  92.3 1.3 convolution_convert_fusion.4
  93.6 3.8 %add_convert_fusion.4 = bf16[512,2048]{1,0:T(8,128)(2,1)S(1)} fusion(bf16[512,2048]{1,0:T(8,128)(2,1)} %bitcast.38, bf16[512,512]{1,0:T(8,128)(2,1)S(1)} %convolution_convert_fusion.4), kind=kOutput, calls=%fused_computation.9 | convolution fusion | flops 1347682304 | bytes 4718592 | tf_op jit(solution)/shard_map/mp,pn->mn/dot_general | solution.py:224
  97.4 1.3 convolution_convert_fusion.3
  98.7 2.9 %add_convert_fusion.3 = bf16[512,2048]{1,0:T(8,128)(2,1)} fusion(bf16[512,2048]{1,0:T(8,128)(2,1)S(1)} %add_convert_fusion.4, bf16[512,512]{1,0:T(8,128)(2,1)S(1)} %convolution_convert_fusion.3), kind=kOutput, calls=%fused_computation.8 | convolution fusion | flops 1347682304 | bytes 4718592 | tf_op jit(solution)/shard_map/mp,pn->mn/dot_general | solution.py:224
  101.6 0.0 copy-start.3
  101.6 3.6 %convolution_convert_fusion.2 = bf16[512,512]{1,0:T(8,128)(2,1)S(1)} fusion(bf16[512,2048]{1,0:T(8,128)(2,1)} %add_convert_fusion.3), kind=kOutput, calls=%fused_computation.27 | convolution fusion | flops 1074003968 | bytes 2621440 | tf_op jit(solution)/shard_map/mn,pn->mp/dot_general | solution.py:221
  105.2 0.0 copy-done.3
  105.2 2.9 %add_convert_fusion.2 = bf16[512,2048]{1,0:T(8,128)(2,1)} fusion(bf16[512,2048]{1,0:T(8,128)(2,1)S(1)} %copy-done.3, bf16[512,512]{1,0:T(8,128)(2,1)S(1)} %convolution_convert_fusion.2), kind=kOutput, calls=%fused_computation.7 | convolution fusion | flops 1347682304 | bytes 4718592 | tf_op jit(solution)/shard_map/mp,pn->mn/dot_general | solution.py:224
  108.1 0.0 copy-start.4
  108.1 3.6 %convolution_convert_fusion.1 = bf16[512,512]{1,0:T(8,128)(2,1)S(1)} fusion(bf16[512,2048]{1,0:T(8,128)(2,1)} %add_convert_fusion.2), kind=kOutput, calls=%fused_computation.26 | convolution fusion | flops 1074003968 | bytes 2621440 | tf_op jit(solution)/shard_map/mn,pn->mp/dot_general | solution.py:221
  111.8 0.0 copy-done.4
  111.8 2.9 %add_convert_fusion.1 = bf16[512,2048]{1,0:T(8,128)(2,1)} fusion(bf16[512,2048]{1,0:T(8,128)(2,1)S(1)} %copy-done.4, bf16[512,512]{1,0:T(8,128)(2,1)S(1)} %convolution_convert_fusion.1), kind=kOutput, calls=%fused_computation.6 | convolution fusion | flops 1347682304 | bytes 4718592 | tf_op jit(solution)/shard_map/mp,pn->mn/dot_general | solution.py:224
  114.7 3.5 %convolution_convert_fusion = bf16[512,512]{1,0:T(8,128)(2,1)S(1)} fusion(bf16[512,2048]{1,0:T(8,128)(2,1)} %add_convert_fusion.1), kind=kOutput, calls=%fused_computation.25 | convolution fusion | flops 1074003968 | bytes 2621440 | tf_op jit(solution)/shard_map/mn,pn->mp/dot_general | solution.py:221
  118.2 3.8 %multiply_convert_fusion = bf16[512,2048]{1,0:T(8,128)(2,1)S(1)} fusion(bf16[512,2048]{1,0:T(8,128)(2,1)} %add_convert_fusion.1, bf16[512,512]{1,0:T(8,128)(2,1)S(1)} %convolution_convert_fusion), kind=kOutput, calls=%fused_computation.4 | convolution fusion | flops 1350828032 | bytes 4718592 | tf_op jit(solution)/shard_map/mp,pn->mn/dot_general | solution.py:224
  122.0 36.6 %giveback.1.ur = bf16[32,16,2048]{2,1,0:T(8,128)(2,1)S(1)} custom-call(bf16[32,16,2048]{2,1,0:T(8,128)(2,1)S(1)} %bitcast.34), custom_call_target="tpu_custom_call" | custom-call | bytes 104857600 | tf_op jit(solution)/shard_map/giveback/pallas_call | solution.py:254
  158.6 0.0 copy-start
  158.6 1.3 copy-done
  159.9 0.0 collective-permute-done.w1p
  159.9 7.3 %finish.1 = (bf16[32,16,2048]{2,1,0:T(8,128)(2,1)}, bf16[32,16,2048]{2,1,0:T(8,128)(2,1)}) custom-call(s32[4,2]{1,0:T(4,128)} %copy-done.1, bf16[32,16,2048]{2,1,0:T(8,128)(2,1)} %get-tuple-element.8.w1, bf16[32,16,2048]{2,1,0:T(8,128)(2,1)} %collective-permute-done.w1p, bf16[32,16,2048]{2,1,0:T(8,128)(2,1)} %copy-done), custom_call_target="tpu_custom_call" | custom-call | tf_op jit(solution)/shard_map/finish/pallas_call | solution.py:267
  167.1 4.7 %copy.11 = f32[1,32,16,2048]{3,2,1,0:T(8,128)} copy(f32[1,32,16,2048]{3,2,1,0:T(8,128)} %bitcast.36) | data formatting | bytes 8388608
Async XLA Ops:
  1.4 85.7 %copy-start.1 = (s32[4,2]{1,0:T(4,128)}, s32[4,2]{1,0:T(4,128)S(1)}, u32[]{:S(2)}) copy-start(s32[4,2]{1,0:T(4,128)S(1)} %copy.9.keep) | copy-start | bytes 100
  87.2 72.7 %collective-permute-start = (bf16[32,16,2048]{2,1,0:T(8,128)(2,1)}, bf16[32,16,2048]{2,1,0:T(8,128)(2,1)}, u32[]{:S(2)}, u32[]{:S(2)}) collective-permute-start(bf16[32,16,2048]{2,1,0:T(8,128)(2,1)} %get-tuple-element.8.w1), channel_id=1, source_target_pairs={{0,64},{32,96},{64,0},{96,32},{1,65},{33,97},{65,1},{97,33},{2,66}... | collective-permute-start | bytes 6291464 | tf_op jit(solution)/shard_map/ppermute | solution.py:251
  91.0 1.3 copy-start.2
  101.6 3.7 %copy-start.3 = (bf16[512,2048]{1,0:T(8,128)(2,1)S(1)}, bf16[512,2048]{1,0:T(8,128)(2,1)}, u32[]{:S(2)}) copy-start(bf16[512,2048]{1,0:T(8,128)(2,1)} %add_convert_fusion.3) | copy-start | bytes 6291460
  108.1 3.7 %copy-start.4 = (bf16[512,2048]{1,0:T(8,128)(2,1)S(1)}, bf16[512,2048]{1,0:T(8,128)(2,1)}, u32[]{:S(2)}) copy-start(bf16[512,2048]{1,0:T(8,128)(2,1)} %add_convert_fusion.2) | copy-start | bytes 6291460
  158.6 1.3 copy-start

commit v3 on v2

v3 whole, which is shorter than its diff:
```python
import functools
import math

import jax
import jax.numpy as jnp
from jax import lax
from jax.experimental import pallas as pl
from jax.experimental.pallas import tpu as pltpu
from jax.sharding import PartitionSpec as P

MESH = pl.DeviceIdType.MESH
NS_STEPS = 5

coeff_a = 3.4445
coeff_b = -4.775
coeff_c = 2.0315
learn_rate = 0.05

STRIDE = 13
HEAD = 8
LAG = 14


def peer_at(me, step, shards):
    return lax.bitwise_xor(me, lax.bitwise_and(step * STRIDE, shards - 1))


LINES = ((1, 2, 3), (8, 16, 24), (4,))


def greet(rep, me, others):
    barrier = pltpu.get_barrier_semaphore()
    near = [(rep, lax.bitwise_xor(me, bits)) for line in LINES for bits in line] + [(other, me) for other in others]
    for device in near:
        pl.semaphore_signal(barrier, inc=1, device_id=device, device_id_type=MESH)
    return lambda: pl.semaphore_wait(barrier, len(near))


def relay(rep, me, line, heard):
    for bits in line:
        pl.semaphore_signal(heard, inc=1, device_id=(rep, lax.bitwise_xor(me, bits)), device_id_type=MESH)
    return lambda: pl.semaphore_wait(heard, len(line))


def shares(keep, rep, bit):
    own = keep[bit, rep].astype(jnp.float32) / 16.0
    return own, 1.0 - own


def dot_nt(a, b):
    return lax.dot_general(a, b, (((1,), (1,)), ((), ())), preferred_element_type=jnp.float32)


def dot_nn(a, b):
    return lax.dot_general(a, b, (((1,), (0,)), ((), ())), preferred_element_type=jnp.float32)


def newton_schulz(x, gram, poly, total):
    size, width = x.shape
    rows = 16
    inverse = 1.0 / (jnp.sqrt(total) + 1e-07)
    update_scale = 0.2 * math.sqrt(max(size, width))

    @pl.loop(0, size // rows)
    def _(i):
        part = pl.ds(pl.multiple_of(i * rows, rows), rows)
        x[part, :] = (x[part, :].astype(jnp.float32) * inverse).astype(jnp.bfloat16)

    @pl.loop(0, NS_STEPS)
    def _(iteration):
        gram[...] = dot_nt(x[...], x[...]).astype(jnp.bfloat16)
        g = gram[...]
        poly[...] = (coeff_b * g.astype(jnp.float32) + coeff_c * dot_nn(g, g)).astype(jnp.bfloat16)
        v = x[...]
        x[...] = (coeff_a * v.astype(jnp.float32) + dot_nn(poly[...], v)).astype(jnp.bfloat16)

    @pl.loop(0, size // rows)
    def _(i):
        part = pl.ds(pl.multiple_of(i * rows, rows), rows)
        x[part, :] = (update_scale * x[part, :].astype(jnp.float32)).astype(jnp.bfloat16)


def step_kernel(
    shards, keep, y, gn, go, w, nt_a, nt_b, nw, update,
    yv, yb, yp, ub, up, gnv, gov, gs, wv, wp, w1v, w1p, nwv, urv, xv, gram, poly,
    y_sem, yb_send, yb_recv, u_send, u_recv, g_send, g_recv, nt_sem, r_send, r_recv, nw_sem, up_sem,
    in_sem, w_send, w_recv, v_send, v_recv, heard_x, heard_y,
):
    rep, me = lax.axis_index("rep"), lax.axis_index("shard")
    core = rep + 1 - 2 * lax.rem(rep, 2)
    side = lax.rem(rep + 2, 4)
    rows = gs.shape[1]
    pieces = v_send.shape[0]
    span = shards // pieces
    enter = greet(rep, me, (core, side))
    at = lambda step: peer_at(me, step, shards)
    block = lambda e: pl.ds(pl.multiple_of(e * rows, rows), rows)

    def load_y(step):
        return pltpu.make_async_copy(y.at[at(step)], yv.at[at(step)], y_sem.at[step])

    def send_y(step):
        e = at(step)
        return pltpu.make_async_remote_copy(
            yb.at[e], yp.at[e], yb_send.at[step], yb_recv.at[step], device_id=(core, me), device_id_type=MESH
        )

    def send_u(step):
        e = at(step)
        return pltpu.make_async_remote_copy(
            ub.at[e], up.at[e], u_send.at[step], u_recv.at[step], device_id=(side, me), device_id_type=MESH
        )

    def send_g(step):
        e = at(step)
        return pltpu.make_async_remote_copy(
            gs.at[e], xv.at[block(me)], g_send.at[step], g_recv.at[step], device_id=(rep, e), device_id_type=MESH
        )

    def send_w1(piece):
        part = pl.ds(piece * span, span)
        return pltpu.make_async_remote_copy(
            w1v.at[part], w1p.at[part], v_send.at[piece], v_recv.at[piece], device_id=(side, me), device_id_type=MESH
        )

    def send_back(step):
        e = at(step)
        return pltpu.make_async_remote_copy(
            xv.at[block(e)], urv.at[me], r_send.at[step], r_recv.at[step], device_id=(rep, e), device_id_type=MESH
        )

    def store_nt(step, half):
        e = at(step)
        width = nt_a.shape[2]
        return pltpu.make_async_copy(
            yv.at[e, :, pl.ds(half * width, width)], (nt_a, nt_b)[half].at[e], nt_sem.at[half, step]
        )

    def store_nw(step):
        return pltpu.make_async_copy(nwv.at[at(step)], nw.at[at(step)], nw_sem.at[step])

    def store_update(step):
        return pltpu.make_async_copy(urv.at[at(step)], update.at[at(step)], up_sem.at[step])

    load_gn = pltpu.make_async_copy(gn, gnv, in_sem.at[0])
    load_go = pltpu.make_async_copy(go, gov, in_sem.at[1])
    load_w = pltpu.make_async_copy(w, wv, in_sem.at[2])
    send_w = pltpu.make_async_remote_copy(wv, wp, w_send, w_recv, device_id=(core, me), device_id_type=MESH)

    @pl.loop(0, shards)
    def _(step):
        load_y(step).start()

    load_gn.start()
    load_go.start()
    load_w.start()
    own0, other0 = shares(keep, rep, 0)
    own1, other1 = shares(keep, rep, 1)

    def narrow(step):
        load_y(step).wait()
        e = at(step)
        yb[e] = yv[e].astype(jnp.bfloat16)

    pl.loop(0, HEAD)(narrow)
    enter()
    all_x = relay(rep, me, LINES[0], heard_x)

    @pl.loop(0, HEAD - 1)
    def _(step):
        send_y(step).start()

    @pl.loop(HEAD, shards + LAG + 1)
    def _(tick):
        @pl.when(tick < shards)
        def _():
            narrow(tick)

        @pl.when((tick >= 1) & (tick <= shards))
        def _():
            send_y(tick - 1).start()

        @pl.when((tick >= LAG) & (tick < shards + LAG))
        def _():
            send_y(tick - LAG).wait_recv()
            e = at(tick - LAG)
            mixed = own0 * yv[e] + other0 * yp[e].astype(jnp.float32)
            yv[e] = mixed
            ub[e] = mixed.astype(jnp.bfloat16)

        @pl.when(tick >= LAG + 1)
        def _():
            send_u(tick - LAG - 1).start()

    all_x()
    all_y = relay(rep, me, LINES[1], heard_y)
    load_w.wait()
    send_w.start()
    all_y()
    load_gn.wait()
    load_go.wait()

    @pl.loop(0, shards + 1)
    def _(tick):
        @pl.when(tick < shards)
        def _():
            send_u(tick).wait_recv()
            e = at(tick)
            fresh = (
                own1 * yv[e] + other1 * up[e].astype(jnp.float32)
                + gnv[e].astype(jnp.float32) - gov[e].astype(jnp.float32)
            )
            yv[e] = fresh
            gs[e] = fresh.astype(jnp.bfloat16)

        @pl.when(tick >= 2)
        def _():
            send_g(tick - 1).start()

        @pl.when(tick >= 1)
        def _():
            store_nt(tick - 1, 0).start()
            store_nt(tick - 1, 1).start()

    send_w.wait()

    @pl.loop(0, shards)
    def _(e):
        w1v[e] = (own0 * wv[e].astype(jnp.float32) + other0 * wp[e].astype(jnp.float32)).astype(jnp.bfloat16)

    xv[block(me), :] = gs[me]

    @pl.loop(0, pieces)
    def _(piece):
        send_w1(piece).start()

    def square(step, total):
        @pl.when(step >= 1)
        def _():
            send_g(step).wait_recv()

        part = xv[block(at(step)), :].astype(jnp.float32)
        return total + part * part

    total = lax.fori_loop(0, shards, square, jnp.zeros((rows, xv.shape[1]), jnp.float32))
    newton_schulz(xv, gram, poly, jnp.sum(total))

    @pl.loop(1, shards)
    def _(step):
        send_back(step).start()

    urv[me] = xv[block(me), :]

    @pl.loop(0, shards)
    def _(step):
        send_y(step).wait_send()
        send_u(step).wait_send()
        store_nt(step, 0).wait()
        store_nt(step, 1).wait()

    @pl.loop(1, shards)
    def _(step):
        send_g(step).wait_send()

    @pl.loop(0, pieces)
    def _(piece):
        send_w1(piece).wait()

    @pl.loop(0, shards)
    def _(e):
        nwv[e] = (own1 * w1v[e].astype(jnp.float32) + other1 * w1p[e].astype(jnp.float32)).astype(jnp.bfloat16)

    @pl.loop(0, shards + 1)
    def _(tick):
        @pl.when(tick < shards)
        def _():
            @pl.when(tick >= 1)
            def _():
                send_back(tick).wait_recv()

            e = at(tick)
            nwv[e] = (nwv[e].astype(jnp.float32) - learn_rate * urv[e].astype(jnp.float32)).astype(jnp.bfloat16)

        @pl.when(tick >= 1)
        def _():
            store_nw(tick - 1).start()
            store_update(tick - 1).start()

    @pl.loop(1, shards)
    def _(step):
        send_back(step).wait_send()

    @pl.loop(0, shards)
    def _(step):
        store_nw(step).wait()
        store_update(step).wait()


def eject_kernel(a, b, c, d, nt, nw, update, sem):
    width = a.shape[2]
    pairs = [(a, nt.at[:, :, pl.ds(0, width)]), (b, nt.at[:, :, pl.ds(width, width)]), (c, nw), (d, update)]
    copies = [pltpu.make_async_copy(x, o, sem.at[i]) for i, (x, o) in enumerate(pairs)]
    for copy in copies:
        copy.start()
    for copy in copies:
        copy.wait()


def local(weight, tracker, grad_new, grad_old, mix_keep):
    shards = lax.axis_size("shard")
    block = weight.shape[1:]
    experts, rows, columns = block
    size = shards * rows
    half = jax.ShapeDtypeStruct(block, jnp.bfloat16)
    full = jax.ShapeDtypeStruct(block, jnp.float32)
    part = jax.ShapeDtypeStruct((experts, rows, columns // 2), jnp.float32)
    anywhere = pl.BlockSpec(memory_space=pl.ANY)
    scalars = pl.BlockSpec(memory_space=pltpu.SMEM)
    dma = pltpu.SemaphoreType.DMA

    made = pl.pallas_call(
        functools.partial(step_kernel, shards),
        out_shape=(part, part, half, half),
        in_specs=[scalars] + [pl.BlockSpec(memory_space=pltpu.HBM)] * 4,
        out_specs=(anywhere,) * 4,
        scratch_shapes=[pltpu.VMEM(block, jnp.float32)] + [pltpu.VMEM(block, jnp.bfloat16)] * 13
        + [pltpu.VMEM((size, columns), jnp.bfloat16)] + [pltpu.VMEM((size, size), jnp.bfloat16)] * 2
        + [dma((shards,))] * 7 + [dma((2, shards))] + [dma((shards,))] * 4 + [dma((3,)), dma, dma, dma((4,)), dma((4,))] + [pltpu.SemaphoreType.REGULAR] * 2,
        compiler_params=pltpu.CompilerParams(collective_id=0, has_side_effects=True, vmem_limit_bytes=48 << 20),
        name="step",
    )(mix_keep.T, tracker[0], grad_new[0], grad_old[0], weight[0])
    new_tracker, new_weight, update = pl.pallas_call(
        eject_kernel,
        out_shape=(full, half, half),
        in_specs=[anywhere] * 4,
        out_specs=(pl.BlockSpec(memory_space=pltpu.HBM),) * 3,
        scratch_shapes=[dma((4,))],
        compiler_params=pltpu.CompilerParams(vmem_limit_bytes=1 << 20),
        name="eject",
    )(*made)
    return (new_weight[None], new_tracker[None], update[None])


def solution(mesh):
    spec = P("rep", None, "shard", None)
    return jax.shard_map(
        local,
        mesh=mesh,
        in_specs=(spec, spec, spec, spec, P()),
        out_specs=(spec, spec, spec),
        check_vma=False,
    )
```

time: 172 us -> 161 us (0.936)
  matrix products: 29.6 us -> 0 us
  Pallas kernels: 130 us -> 156 us
  local copies, waits for them, and re-layouts: 8.1 us -> 3.85 us
  other arithmetic: 2.08 us -> 0 us
    dot_general x10 -> x0, matrix products: 29.6 us -> none  [the longest x5 16.2 us: orthogonalize(): jnp.einsum('mp,pn->mn', polynomial, iterate, preferred_element_type=jnp.f...]
    pallas_call x3 -> x2, Pallas kernels: 130 us -> 156 us  [the longest x1 152 us: local(): pl.pallas_call(functools.partial(step_kernel, shards), out_shape=(part, p...]
    unnamed x12 -> x6, local copies, waits for them, and re-layouts: 8.1 us -> 3.85 us
  transfers between devices with their start and end apart: 1 -> 0, of which waited for: 0 -> 0; matrix products, arithmetic and copies ran while one was open for 18% -> 0% of each run, Pallas kernels for 21% -> 0%
where the time goes in v3:
time: 161 us; the launch traced here: 160 us
  Pallas kernels  156 us (97%)
  local copies, waits for them, and re-layouts  3.85 us (2%)
    pallas_call x1, Pallas kernels, local(): pl.pallas_call(functools.partial(step_kernel, shards), out_shape=(part, p...  152 us
    unnamed x6, local copies, waits for them, and re-layouts  3.85 us
    pallas_call x1, Pallas kernels, local(): pl.pallas_call(eject_kernel, out_shape=(full, half, half), in_specs=[anyw...  3.36 us

profile of v3, /device:TPU:0, one launch (start us, length us, event | category | flops | bytes accessed | tf_op | source)
XLA Modules:
  0.0 160.1 jit_solution(16322091482986518790)
XLA Ops:
  0.6 0.0 copy-start.2
  0.6 0.7 copy-done.2
  1.3 152.3 %step.1 = (f32[32,16,1024]{2,1,0:T(8,128)S(1)}, f32[32,16,1024]{2,1,0:T(8,128)S(1)}, bf16[32,16,2048]{2,1,0:T(8,128)(2,1)}, bf16[32,16,2048]{2,1,0:T(8,128)(2,1)}) custom-call(s32[2,4]{1,0:T(2,128)S(1)} %bitcast.8, f32[32,16,2048]{2,1,0:T(8,128)} %bitcast.9, bf16[32,16,2048]{2,1,0:T(8,128)(2,1)} %bitcast.10, bf16[32,16,2048]{2,1,0:T(8,128)(2,1)} %bitcast.11, ...), custom_call_target="tpu_custom_call" | custom-call | tf_op jit(solution)/shard_map/step/pallas_call | solution.py:321
  153.6 0.0 copy-start
  153.6 1.6 copy-done
  155.2 0.0 copy-start.1
  155.2 1.6 copy-done.1
  156.8 3.4 %eject.1 = (f32[32,16,2048]{2,1,0:T(8,128)}, bf16[32,16,2048]{2,1,0:T(8,128)(2,1)}, bf16[32,16,2048]{2,1,0:T(8,128)(2,1)}) custom-call(f32[32,16,1024]{2,1,0:T(8,128)S(1)} %get-tuple-element.10.a, f32[32,16,1024]{2,1,0:T(8,128)S(1)} %get-tuple-element.11.b, bf16[32,16,2048]{2,1,0:T(8,128)(2,1)S(1)} %copy-done, bf16[32,16,2048]{2,1,0:T(8,128)(2,1)S(1)} %copy-done.1), custom_call_target="tpu_custom_call" | custom-call | tf_op jit(solution)/shard_map/eject/pallas_call | solution.py:332
Async XLA Ops:
  0.6 0.7 copy-start.2
  153.6 1.6 copy-start
  155.2 1.6 copy-start.1

commit v4 on v3

--- a/solution.py
+++ b/solution.py
@@ -19,6 +19,7 @@
 STRIDE = 13
 HEAD = 8
 LAG = 14
+AHEAD = 4
 
 
 def peer_at(me, step, shards):
@@ -81,23 +82,24 @@
 
 
 def step_kernel(
-    shards, keep, y, gn, go, w, nt_a, nt_b, nw, update,
-    yv, yb, yp, ub, up, gnv, gov, gs, wv, wp, w1v, w1p, nwv, urv, xv, gram, poly,
-    y_sem, yb_send, yb_recv, u_send, u_recv, g_send, g_recv, nt_sem, r_send, r_recv, nw_sem, up_sem,
-    in_sem, w_send, w_recv, v_send, v_recv, heard_x, heard_y,
+    shards, keep, y, gn, go, w, nt, nw, update,
+    yb, yp, ub, up, gnv, gov, gs, wv, wp, w1v, w1p, wz, wzp, xv, gram, poly,
+    y_sem, yb_send, yb_recv, u_send, u_recv, g_send, g_recv, r_send, r_recv,
+    in_sem, w_send, w_recv, v_send, v_recv, heard_x, heard_y, ahead_sem,
 ):
     rep, me = lax.axis_index("rep"), lax.axis_index("shard")
     core = rep + 1 - 2 * lax.rem(rep, 2)
     side = lax.rem(rep + 2, 4)
     rows = gs.shape[1]
     pieces = v_send.shape[0]
-    span = shards // pieces
+    ahead = wz.shape[0]
+    span = (shards - ahead) // pieces
     enter = greet(rep, me, (core, side))
     at = lambda step: peer_at(me, step, shards)
     block = lambda e: pl.ds(pl.multiple_of(e * rows, rows), rows)
 
     def load_y(step):
-        return pltpu.make_async_copy(y.at[at(step)], yv.at[at(step)], y_sem.at[step])
+        return pltpu.make_async_copy(y.at[at(step)], nt.at[at(step)], y_sem.at[step])
 
     def send_y(step):
         e = at(step)
@@ -118,7 +120,7 @@
         )
 
     def send_w1(piece):
-        part = pl.ds(piece * span, span)
+        part = pl.ds(ahead + piece * span, span)
         return pltpu.make_async_remote_copy(
             w1v.at[part], w1p.at[part], v_send.at[piece], v_recv.at[piece], device_id=(side, me), device_id_type=MESH
         )
@@ -126,26 +128,20 @@
     def send_back(step):
         e = at(step)
         return pltpu.make_async_remote_copy(
-            xv.at[block(e)], urv.at[me], r_send.at[step], r_recv.at[step], device_id=(rep, e), device_id_type=MESH
-        )
-
-    def store_nt(step, half):
-        e = at(step)
-        width = nt_a.shape[2]
-        return pltpu.make_async_copy(
-            yv.at[e, :, pl.ds(half * width, width)], (nt_a, nt_b)[half].at[e], nt_sem.at[half, step]
-        )
-
-    def store_nw(step):
-        return pltpu.make_async_copy(nwv.at[at(step)], nw.at[at(step)], nw_sem.at[step])
-
-    def store_update(step):
-        return pltpu.make_async_copy(urv.at[at(step)], update.at[at(step)], up_sem.at[step])
+            xv.at[block(e)], update.at[me], r_send.at[step], r_recv.at[step], device_id=(rep, e), device_id_type=MESH
+        )
 
     load_gn = pltpu.make_async_copy(gn, gnv, in_sem.at[0])
     load_go = pltpu.make_async_copy(go, gov, in_sem.at[1])
     load_w = pltpu.make_async_copy(w, wv, in_sem.at[2])
     send_w = pltpu.make_async_remote_copy(wv, wp, w_send, w_recv, device_id=(core, me), device_id_type=MESH)
+
+    early = pltpu.make_async_remote_copy(
+        w.at[pl.ds(0, ahead)], wz, ahead_sem.at[0], ahead_sem.at[1], device_id=(side, me), device_id_type=MESH
+    )
+    early_across = pltpu.make_async_remote_copy(
+        wz, wzp, ahead_sem.at[2], ahead_sem.at[3], device_id=(core, me), device_id_type=MESH
+    )
 
     @pl.loop(0, shards)
     def _(step):
@@ -160,10 +156,11 @@
     def narrow(step):
         load_y(step).wait()
         e = at(step)
-        yb[e] = yv[e].astype(jnp.bfloat16)
+        yb[e] = nt[e].astype(jnp.bfloat16)
 
     pl.loop(0, HEAD)(narrow)
     enter()
+    early.start()
     all_x = relay(rep, me, LINES[0], heard_x)
 
     @pl.loop(0, HEAD - 1)
@@ -184,8 +181,8 @@
         def _():
             send_y(tick - LAG).wait_recv()
             e = at(tick - LAG)
-            mixed = own0 * yv[e] + other0 * yp[e].astype(jnp.float32)
-            yv[e] = mixed
+            mixed = own0 * nt[e] + other0 * yp[e].astype(jnp.float32)
+            nt[e] = mixed
             ub[e] = mixed.astype(jnp.bfloat16)
 
         @pl.when(tick >= LAG + 1)
@@ -207,22 +204,19 @@
             send_u(tick).wait_recv()
             e = at(tick)
             fresh = (
-                own1 * yv[e] + other1 * up[e].astype(jnp.float32)
+                own1 * nt[e] + other1 * up[e].astype(jnp.float32)
                 + gnv[e].astype(jnp.float32) - gov[e].astype(jnp.float32)
             )
-            yv[e] = fresh
+            nt[e] = fresh
             gs[e] = fresh.astype(jnp.bfloat16)
 
         @pl.when(tick >= 2)
         def _():
             send_g(tick - 1).start()
 
-        @pl.when(tick >= 1)
-        def _():
-            store_nt(tick - 1, 0).start()
-            store_nt(tick - 1, 1).start()
-
     send_w.wait()
+    early.wait()
+    early_across.start()
 
     @pl.loop(0, shards)
     def _(e):
@@ -249,18 +243,23 @@
     def _(step):
         send_back(step).start()
 
-    urv[me] = xv[block(me), :]
+    update[me] = xv[block(me), :]
 
     @pl.loop(0, shards)
     def _(step):
         send_y(step).wait_send()
         send_u(step).wait_send()
-        store_nt(step, 0).wait()
-        store_nt(step, 1).wait()
 
     @pl.loop(1, shards)
     def _(step):
         send_g(step).wait_send()
+
+    early_across.wait()
+    side_own0, side_other0 = shares(keep, side, 0)
+
+    @pl.loop(0, ahead)
+    def _(e):
+        w1p[e] = (side_own0 * wz[e].astype(jnp.float32) + side_other0 * wzp[e].astype(jnp.float32)).astype(jnp.bfloat16)
 
     @pl.loop(0, pieces)
     def _(piece):
@@ -268,38 +267,24 @@
 
     @pl.loop(0, shards)
     def _(e):
-        nwv[e] = (own1 * w1v[e].astype(jnp.float32) + other1 * w1p[e].astype(jnp.float32)).astype(jnp.bfloat16)
-
-    @pl.loop(0, shards + 1)
-    def _(tick):
-        @pl.when(tick < shards)
-        def _():
-            @pl.when(tick >= 1)
-            def _():
-                send_back(tick).wait_recv()
-
-            e = at(tick)
-            nwv[e] = (nwv[e].astype(jnp.float32) - learn_rate * urv[e].astype(jnp.float32)).astype(jnp.bfloat16)
-
-        @pl.when(tick >= 1)
-        def _():
-            store_nw(tick - 1).start()
-            store_update(tick - 1).start()
+        nw[e] = (own1 * w1v[e].astype(jnp.float32) + other1 * w1p[e].astype(jnp.float32)).astype(jnp.bfloat16)
+
+    @pl.loop(0, shards)
+    def _(step):
+        @pl.when(step >= 1)
+        def _():
+            send_back(step).wait_recv()
+
+        e = at(step)
+        nw[e] = (nw[e].astype(jnp.float32) - learn_rate * update[e].astype(jnp.float32)).astype(jnp.bfloat16)
 
     @pl.loop(1, shards)
     def _(step):
         send_back(step).wait_send()
 
-    @pl.loop(0, shards)
-    def _(step):
-        store_nw(step).wait()
-        store_update(step).wait()
-
-
-def eject_kernel(a, b, c, d, nt, nw, update, sem):
-    width = a.shape[2]
-    pairs = [(a, nt.at[:, :, pl.ds(0, width)]), (b, nt.at[:, :, pl.ds(width, width)]), (c, nw), (d, update)]
-    copies = [pltpu.make_async_copy(x, o, sem.at[i]) for i, (x, o) in enumerate(pairs)]
+
+def eject_kernel(a, b, c, nt, nw, update, sem):
+    copies = [pltpu.make_async_copy(x, o, sem.at[i]) for i, (x, o) in enumerate([(a, nt), (b, nw), (c, update)])]
     for copy in copies:
         copy.start()
     for copy in copies:
@@ -313,28 +298,28 @@
     size = shards * rows
     half = jax.ShapeDtypeStruct(block, jnp.bfloat16)
     full = jax.ShapeDtypeStruct(block, jnp.float32)
-    part = jax.ShapeDtypeStruct((experts, rows, columns // 2), jnp.float32)
     anywhere = pl.BlockSpec(memory_space=pl.ANY)
     scalars = pl.BlockSpec(memory_space=pltpu.SMEM)
     dma = pltpu.SemaphoreType.DMA
 
     made = pl.pallas_call(
         functools.partial(step_kernel, shards),
-        out_shape=(part, part, half, half),
+        out_shape=(pltpu.VMEM(block, jnp.float32), pltpu.VMEM(block, jnp.bfloat16), pltpu.VMEM(block, jnp.bfloat16)),
         in_specs=[scalars] + [pl.BlockSpec(memory_space=pltpu.HBM)] * 4,
-        out_specs=(anywhere,) * 4,
-        scratch_shapes=[pltpu.VMEM(block, jnp.float32)] + [pltpu.VMEM(block, jnp.bfloat16)] * 13
+        out_specs=(pl.BlockSpec(memory_space=pltpu.VMEM),) * 3,
+        scratch_shapes=[pltpu.VMEM(block, jnp.bfloat16)] * 11
+        + [pltpu.VMEM((AHEAD, rows, columns), jnp.bfloat16)] * 2
         + [pltpu.VMEM((size, columns), jnp.bfloat16)] + [pltpu.VMEM((size, size), jnp.bfloat16)] * 2
-        + [dma((shards,))] * 7 + [dma((2, shards))] + [dma((shards,))] * 4 + [dma((3,)), dma, dma, dma((4,)), dma((4,))] + [pltpu.SemaphoreType.REGULAR] * 2,
+        + [dma((shards,))] * 9 + [dma((3,)), dma, dma, dma((4,)), dma((4,))] + [pltpu.SemaphoreType.REGULAR] * 2 + [dma((4,))],
         compiler_params=pltpu.CompilerParams(collective_id=0, has_side_effects=True, vmem_limit_bytes=48 << 20),
         name="step",
     )(mix_keep.T, tracker[0], grad_new[0], grad_old[0], weight[0])
     new_tracker, new_weight, update = pl.pallas_call(
         eject_kernel,
         out_shape=(full, half, half),
-        in_specs=[anywhere] * 4,
+        in_specs=[pl.BlockSpec(memory_space=pltpu.VMEM)] * 3,
         out_specs=(pl.BlockSpec(memory_space=pltpu.HBM),) * 3,
-        scratch_shapes=[dma((4,))],
+        scratch_shapes=[dma((3,))],
         compiler_params=pltpu.CompilerParams(vmem_limit_bytes=1 << 20),
         name="eject",
     )(*made)

time: 161 us -> 152 us (0.944)
  Pallas kernels: 156 us -> 151 us
  local copies, waits for them, and re-layouts: 3.85 us -> 0 us
    pallas_call x2, Pallas kernels: 156 us -> 151 us  [the longest x1 148 us: local(): pl.pallas_call(functools.partial(step_kernel, shards), out_shape=(pltpu.V...]
    unnamed x6 -> x0, local copies, waits for them, and re-layouts: 3.85 us -> none
where the time goes in v4:
time: 152 us
  Pallas kernels  151 us (99%)
    pallas_call x1, Pallas kernels, local(): pl.pallas_call(functools.partial(step_kernel, shards), out_shape=(pltpu.V...  148 us
    pallas_call x1, Pallas kernels, local(): pl.pallas_call(eject_kernel, out_shape=(full, half, half), in_specs=[pl.B...  3.36 us

profile of v4, /device:TPU:0, one launch (start us, length us, event | category | flops | bytes accessed | tf_op | source)
XLA Modules:
  0.0 151.6 jit_solution(4044605606073206197)
XLA Ops:
  0.6 147.6 %step.1 = (f32[32,16,2048]{2,1,0:T(8,128)S(1)}, bf16[32,16,2048]{2,1,0:T(8,128)(2,1)S(1)}, bf16[32,16,2048]{2,1,0:T(8,128)(2,1)S(1)}) custom-call(s32[2,4]{1,0:T(2,128)} %bitcast.12, f32[32,16,2048]{2,1,0:T(8,128)} %bitcast.8, bf16[32,16,2048]{2,1,0:T(8,128)(2,1)} %bitcast.9, bf16[32,16,2048]{2,1,0:T(8,128)(2,1)} %bitcast.10, bf16[32,16,2048]{2,1,0:T(8,128)(2,1)} %bitcast.11), custom_call_target="tpu_custom_call" | custom-call | tf_op jit(solution)/shard_map/step/pallas_call | solution.py:305
  148.3 3.4 %eject.1 = (f32[32,16,2048]{2,1,0:T(8,128)}, bf16[32,16,2048]{2,1,0:T(8,128)(2,1)}, bf16[32,16,2048]{2,1,0:T(8,128)(2,1)}) custom-call(f32[32,16,2048]{2,1,0:T(8,128)S(1)} %get-tuple-element.9.a, bf16[32,16,2048]{2,1,0:T(8,128)(2,1)S(1)} %get-tuple-element.10.b, bf16[32,16,2048]{2,1,0:T(8,128)(2,1)S(1)} %get-tuple-element.11.c), custom_call_target="tpu_custom_call" | custom-call | tf_op jit(solution)/shard_map/eject/pallas_call | solution.py:317

commit v5 on v4

--- a/solution.py
+++ b/solution.py
@@ -20,6 +20,7 @@
 HEAD = 8
 LAG = 14
 AHEAD = 4
+LATE = 8
 
 
 def peer_at(me, step, shards):
@@ -85,7 +86,7 @@
     shards, keep, y, gn, go, w, nt, nw, update,
     yb, yp, ub, up, gnv, gov, gs, wv, wp, w1v, w1p, wz, wzp, xv, gram, poly,
     y_sem, yb_send, yb_recv, u_send, u_recv, g_send, g_recv, r_send, r_recv,
-    in_sem, w_send, w_recv, v_send, v_recv, heard_x, heard_y, ahead_sem,
+    in_sem, w_send, w_recv, v_send, v_recv, heard_x, heard_y, ahead_sem, l_send, l_recv,
 ):
     rep, me = lax.axis_index("rep"), lax.axis_index("shard")
     core = rep + 1 - 2 * lax.rem(rep, 2)
@@ -93,7 +94,9 @@
     rows = gs.shape[1]
     pieces = v_send.shape[0]
     ahead = wz.shape[0]
-    span = (shards - ahead) // pieces
+    late = l_send.shape[0]
+    first_late = shards - late
+    span = (first_late - ahead) // pieces
     enter = greet(rep, me, (core, side))
     at = lambda step: peer_at(me, step, shards)
     block = lambda e: pl.ds(pl.multiple_of(e * rows, rows), rows)
@@ -123,6 +126,12 @@
         part = pl.ds(ahead + piece * span, span)
         return pltpu.make_async_remote_copy(
             w1v.at[part], w1p.at[part], v_send.at[piece], v_recv.at[piece], device_id=(side, me), device_id_type=MESH
+        )
+
+    def send_late(i):
+        e = first_late + i
+        return pltpu.make_async_remote_copy(
+            w1v.at[e], w1p.at[e], l_send.at[i], l_recv.at[i], device_id=(side, me), device_id_type=MESH
         )
 
     def send_back(step):
@@ -158,9 +167,9 @@
         e = at(step)
         yb[e] = nt[e].astype(jnp.bfloat16)
 
-    pl.loop(0, HEAD)(narrow)
     enter()
     early.start()
+    pl.loop(0, HEAD)(narrow)
     all_x = relay(rep, me, LINES[0], heard_x)
 
     @pl.loop(0, HEAD - 1)
@@ -243,6 +252,10 @@
     def _(step):
         send_back(step).start()
 
+    @pl.loop(0, late)
+    def _(i):
+        send_late(i).start()
+
     update[me] = xv[block(me), :]
 
     @pl.loop(0, shards)
@@ -265,18 +278,33 @@
     def _(piece):
         send_w1(piece).wait()
 
+    def mixed_weight(e):
+        return (own1 * w1v[e].astype(jnp.float32) + other1 * w1p[e].astype(jnp.float32)).astype(jnp.bfloat16)
+
+    def stepped(mixed, e):
+        return (mixed.astype(jnp.float32) - learn_rate * update[e].astype(jnp.float32)).astype(jnp.bfloat16)
+
+    @pl.loop(0, first_late)
+    def _(e):
+        nw[e] = mixed_weight(e)
+
     @pl.loop(0, shards)
-    def _(e):
-        nw[e] = (own1 * w1v[e].astype(jnp.float32) + other1 * w1p[e].astype(jnp.float32)).astype(jnp.bfloat16)
-
-    @pl.loop(0, shards)
     def _(step):
         @pl.when(step >= 1)
         def _():
             send_back(step).wait_recv()
 
         e = at(step)
-        nw[e] = (nw[e].astype(jnp.float32) - learn_rate * update[e].astype(jnp.float32)).astype(jnp.bfloat16)
+
+        @pl.when(e < first_late)
+        def _():
+            nw[e] = stepped(nw[e], e)
+
+    @pl.loop(0, late)
+    def _(i):
+        send_late(i).wait()
+        e = first_late + i
+        nw[e] = stepped(mixed_weight(e), e)
 
     @pl.loop(1, shards)
     def _(step):
@@ -310,7 +338,7 @@
         scratch_shapes=[pltpu.VMEM(block, jnp.bfloat16)] * 11
         + [pltpu.VMEM((AHEAD, rows, columns), jnp.bfloat16)] * 2
         + [pltpu.VMEM((size, columns), jnp.bfloat16)] + [pltpu.VMEM((size, size), jnp.bfloat16)] * 2
-        + [dma((shards,))] * 9 + [dma((3,)), dma, dma, dma((4,)), dma((4,))] + [pltpu.SemaphoreType.REGULAR] * 2 + [dma((4,))],
+        + [dma((shards,))] * 9 + [dma((3,)), dma, dma, dma((4,)), dma((4,))] + [pltpu.SemaphoreType.REGULAR] * 2 + [dma((4,))] + [dma((LATE,))] * 2,
         compiler_params=pltpu.CompilerParams(collective_id=0, has_side_effects=True, vmem_limit_bytes=48 << 20),
         name="step",
     )(mix_keep.T, tracker[0], grad_new[0], grad_old[0], weight[0])

time: 152 us -> 149 us (0.980)
  Pallas kernels: 151 us -> 148 us
    pallas_call x1, Pallas kernels: 148 us -> 145 us  [local(): pl.pallas_call(functools.partial(step_kernel, shards), out_shape=(pltpu.V...]
where the time goes in v5:
time: 149 us
  Pallas kernels  148 us (99%)
    pallas_call x1, Pallas kernels, local(): pl.pallas_call(functools.partial(step_kernel, shards), out_shape=(pltpu.V...  145 us
    pallas_call x1, Pallas kernels, local(): pl.pallas_call(eject_kernel, out_shape=(full, half, half), in_specs=[pl.B...  3.36 us

profile of v5, /device:TPU:0, one launch (start us, length us, event | category | flops | bytes accessed | tf_op | source)
XLA Modules:
  0.0 148.6 jit_solution(11937238123585036978)
XLA Ops:
  0.6 144.6 %step.1 = (f32[32,16,2048]{2,1,0:T(8,128)S(1)}, bf16[32,16,2048]{2,1,0:T(8,128)(2,1)S(1)}, bf16[32,16,2048]{2,1,0:T(8,128)(2,1)S(1)}) custom-call(s32[2,4]{1,0:T(2,128)} %bitcast.12, f32[32,16,2048]{2,1,0:T(8,128)} %bitcast.8, bf16[32,16,2048]{2,1,0:T(8,128)(2,1)} %bitcast.9, bf16[32,16,2048]{2,1,0:T(8,128)(2,1)} %bitcast.10, bf16[32,16,2048]{2,1,0:T(8,128)(2,1)} %bitcast.11), custom_call_target="tpu_custom_call" | custom-call | tf_op jit(solution)/shard_map/step/pallas_call | solution.py:333
  145.2 3.4 %eject.1 = (f32[32,16,2048]{2,1,0:T(8,128)}, bf16[32,16,2048]{2,1,0:T(8,128)(2,1)}, bf16[32,16,2048]{2,1,0:T(8,128)(2,1)}) custom-call(f32[32,16,2048]{2,1,0:T(8,128)S(1)} %get-tuple-element.9.a, bf16[32,16,2048]{2,1,0:T(8,128)(2,1)S(1)} %get-tuple-element.10.b, bf16[32,16,2048]{2,1,0:T(8,128)(2,1)S(1)} %get-tuple-element.11.c), custom_call_target="tpu_custom_call" | custom-call | tf_op jit(solution)/shard_map/eject/pallas_call | solution.py:345

commit v6 on v5

--- a/solution.py
+++ b/solution.py
@@ -21,6 +21,8 @@
 LAG = 14
 AHEAD = 4
 LATE = 8
+GROUP = 4
+SENDS = 8
 
 
 def peer_at(me, step, shards):
@@ -102,24 +104,24 @@
     block = lambda e: pl.ds(pl.multiple_of(e * rows, rows), rows)
 
     def load_y(step):
-        return pltpu.make_async_copy(y.at[at(step)], nt.at[at(step)], y_sem.at[step])
+        return pltpu.make_async_copy(y.at[at(step)], nt.at[at(step)], y_sem.at[lax.div(step, GROUP)])
 
     def send_y(step):
         e = at(step)
         return pltpu.make_async_remote_copy(
-            yb.at[e], yp.at[e], yb_send.at[step], yb_recv.at[step], device_id=(core, me), device_id_type=MESH
+            yb.at[e], yp.at[e], yb_send.at[lax.div(step, SENDS)], yb_recv.at[lax.div(step, GROUP)], device_id=(core, me), device_id_type=MESH
         )
 
     def send_u(step):
         e = at(step)
         return pltpu.make_async_remote_copy(
-            ub.at[e], up.at[e], u_send.at[step], u_recv.at[step], device_id=(side, me), device_id_type=MESH
+            ub.at[e], up.at[e], u_send.at[lax.div(step, SENDS)], u_recv.at[lax.div(step, GROUP)], device_id=(side, me), device_id_type=MESH
         )
 
     def send_g(step):
         e = at(step)
         return pltpu.make_async_remote_copy(
-            gs.at[e], xv.at[block(me)], g_send.at[step], g_recv.at[step], device_id=(rep, e), device_id_type=MESH
+            gs.at[e], xv.at[block(me)], g_send.at[lax.div(step, SENDS)], g_recv.at[lax.div(step, GROUP)], device_id=(rep, e), device_id_type=MESH
         )
 
     def send_w1(piece):
@@ -137,8 +139,35 @@
     def send_back(step):
         e = at(step)
         return pltpu.make_async_remote_copy(
-            xv.at[block(e)], update.at[me], r_send.at[step], r_recv.at[step], device_id=(rep, e), device_id_type=MESH
-        )
+            xv.at[block(e)], update.at[me], r_send.at[step], r_recv.at[lax.div(step, GROUP)], device_id=(rep, e), device_id_type=MESH
+        )
+
+    def awaited(blocks, sent, received):
+        return pltpu.make_async_remote_copy(
+            blocks, blocks, sent, received, device_id=(core, me), device_id_type=MESH
+        )
+
+    def arrived(blocks, semaphore, step, missing):
+        group = lax.div(step, GROUP)
+        size = blocks.shape[0] // shards
+
+        def wait(count):
+            awaited(blocks.at[pl.ds(0, count * size)], y_sem.at[0], semaphore.at[group]).wait_recv()
+
+        if missing:
+            pl.when(step == 0)(lambda: wait(GROUP - missing))
+            pl.when((step > 0) & (lax.rem(step, GROUP) == 0))(lambda: wait(GROUP))
+        else:
+            pl.when(lax.rem(step, GROUP) == 0)(lambda: wait(GROUP))
+
+    def all_sent(blocks, semaphore, missing):
+        size = blocks.shape[0] // shards
+        if missing:
+            awaited(blocks.at[pl.ds(0, (SENDS - missing) * size)], semaphore.at[0], y_sem.at[0]).wait_send()
+
+        @pl.loop(1 if missing else 0, shards // SENDS)
+        def _(group):
+            awaited(blocks.at[pl.ds(0, SENDS * size)], semaphore.at[group], y_sem.at[0]).wait_send()
 
     load_gn = pltpu.make_async_copy(gn, gnv, in_sem.at[0])
     load_go = pltpu.make_async_copy(go, gov, in_sem.at[1])
@@ -163,7 +192,11 @@
     own1, other1 = shares(keep, rep, 1)
 
     def narrow(step):
-        load_y(step).wait()
+        @pl.when(lax.rem(step, GROUP) == 0)
+        def _():
+            part = pl.ds(0, GROUP)
+            pltpu.make_async_copy(y.at[part], nt.at[part], y_sem.at[lax.div(step, GROUP)]).wait()
+
         e = at(step)
         yb[e] = nt[e].astype(jnp.bfloat16)
 
@@ -188,7 +221,7 @@
 
         @pl.when((tick >= LAG) & (tick < shards + LAG))
         def _():
-            send_y(tick - LAG).wait_recv()
+            arrived(yp, yb_recv, tick - LAG, 0)
             e = at(tick - LAG)
             mixed = own0 * nt[e] + other0 * yp[e].astype(jnp.float32)
             nt[e] = mixed
@@ -210,7 +243,7 @@
     def _(tick):
         @pl.when(tick < shards)
         def _():
-            send_u(tick).wait_recv()
+            arrived(up, u_recv, tick, 0)
             e = at(tick)
             fresh = (
                 own1 * nt[e] + other1 * up[e].astype(jnp.float32)
@@ -238,10 +271,7 @@
         send_w1(piece).start()
 
     def square(step, total):
-        @pl.when(step >= 1)
-        def _():
-            send_g(step).wait_recv()
-
+        arrived(xv, g_recv, step, 1)
         part = xv[block(at(step)), :].astype(jnp.float32)
         return total + part * part
 
@@ -258,14 +288,7 @@
 
     update[me] = xv[block(me), :]
 
-    @pl.loop(0, shards)
-    def _(step):
-        send_y(step).wait_send()
-        send_u(step).wait_send()
-
-    @pl.loop(1, shards)
-    def _(step):
-        send_g(step).wait_send()
+    all_sent(gs, g_send, 1)
 
     early_across.wait()
     side_own0, side_other0 = shares(keep, side, 0)
@@ -274,6 +297,10 @@
     def _(e):
         w1p[e] = (side_own0 * wz[e].astype(jnp.float32) + side_other0 * wzp[e].astype(jnp.float32)).astype(jnp.bfloat16)
 
+    all_sent(yb, yb_send, 0)
+
+    all_sent(ub, u_send, 0)
+
     @pl.loop(0, pieces)
     def _(piece):
         send_w1(piece).wait()
@@ -290,25 +317,22 @@
 
     @pl.loop(0, shards)
     def _(step):
-        @pl.when(step >= 1)
-        def _():
-            send_back(step).wait_recv()
-
+        arrived(update, r_recv, step, 1)
         e = at(step)
 
         @pl.when(e < first_late)
         def _():
             nw[e] = stepped(nw[e], e)
+
+    @pl.loop(1, shards)
+    def _(step):
+        send_back(step).wait_send()
 
     @pl.loop(0, late)
     def _(i):
         send_late(i).wait()
         e = first_late + i
         nw[e] = stepped(mixed_weight(e), e)
-
-    @pl.loop(1, shards)
-    def _(step):
-        send_back(step).wait_send()
 
 
 def eject_kernel(a, b, c, nt, nw, update, sem):
@@ -338,7 +362,7 @@
         scratch_shapes=[pltpu.VMEM(block, jnp.bfloat16)] * 11
         + [pltpu.VMEM((AHEAD, rows, columns), jnp.bfloat16)] * 2
         + [pltpu.VMEM((size, columns), jnp.bfloat16)] + [pltpu.VMEM((size, size), jnp.bfloat16)] * 2
-        + [dma((shards,))] * 9 + [dma((3,)), dma, dma, dma((4,)), dma((4,))] + [pltpu.SemaphoreType.REGULAR] * 2 + [dma((4,))] + [dma((LATE,))] * 2,
+        + [dma((shards // GROUP,)), dma((shards // SENDS,)), dma((shards // GROUP,)), dma((shards // SENDS,)), dma((shards // GROUP,)), dma((shards // SENDS,)), dma((shards // GROUP,)), dma((shards,)), dma((shards // GROUP,))] + [dma((3,)), dma, dma, dma((4,)), dma((4,))] + [pltpu.SemaphoreType.REGULAR] * 2 + [dma((4,))] + [dma((LATE,))] * 2,
         compiler_params=pltpu.CompilerParams(collective_id=0, has_side_effects=True, vmem_limit_bytes=48 << 20),
         name="step",
     )(mix_keep.T, tracker[0], grad_new[0], grad_old[0], weight[0])

time: 149 us -> 147 us (0.987)
  Pallas kernels: 148 us -> 146 us
    pallas_call x1, Pallas kernels: 145 us -> 143 us  [local(): pl.pallas_call(functools.partial(step_kernel, shards), out_shape=(pltpu.V...]
where the time goes in v6:
time: 147 us
  Pallas kernels  146 us (99%)
    pallas_call x1, Pallas kernels, local(): pl.pallas_call(functools.partial(step_kernel, shards), out_shape=(pltpu.V...  143 us
    pallas_call x1, Pallas kernels, local(): pl.pallas_call(eject_kernel, out_shape=(full, half, half), in_specs=[pl.B...  3.36 us

profile of v6, /device:TPU:0, one launch (start us, length us, event | category | flops | bytes accessed | tf_op | source)
XLA Modules:
  0.0 146.6 jit_solution(212284755923118134)
XLA Ops:
  0.6 142.6 %step.1 = (f32[32,16,2048]{2,1,0:T(8,128)S(1)}, bf16[32,16,2048]{2,1,0:T(8,128)(2,1)S(1)}, bf16[32,16,2048]{2,1,0:T(8,128)(2,1)S(1)}) custom-call(s32[2,4]{1,0:T(2,128)} %bitcast.12, f32[32,16,2048]{2,1,0:T(8,128)} %bitcast.8, bf16[32,16,2048]{2,1,0:T(8,128)(2,1)} %bitcast.9, bf16[32,16,2048]{2,1,0:T(8,128)(2,1)} %bitcast.10, bf16[32,16,2048]{2,1,0:T(8,128)(2,1)} %bitcast.11), custom_call_target="tpu_custom_call" | custom-call | tf_op jit(solution)/shard_map/step/pallas_call | solution.py:357
  143.2 3.4 %eject.1 = (f32[32,16,2048]{2,1,0:T(8,128)}, bf16[32,16,2048]{2,1,0:T(8,128)(2,1)}, bf16[32,16,2048]{2,1,0:T(8,128)(2,1)}) custom-call(f32[32,16,2048]{2,1,0:T(8,128)S(1)} %get-tuple-element.9.a, bf16[32,16,2048]{2,1,0:T(8,128)(2,1)S(1)} %get-tuple-element.10.b, bf16[32,16,2048]{2,1,0:T(8,128)(2,1)S(1)} %get-tuple-element.11.c), custom_call_target="tpu_custom_call" | custom-call | tf_op jit(solution)/shard_map/eject/pallas_call | solution.py:369

commit v7 on v6

--- a/solution.py
+++ b/solution.py
@@ -21,7 +21,7 @@
 LAG = 14
 AHEAD = 4
 LATE = 8
-GROUP = 4
+GROUP = 8
 SENDS = 8
 
 

time: 147 us -> 147 us (level)
  no operation moved by 1% of the time
where the time goes in v7:
time: 147 us
  Pallas kernels  146 us (99%)
    pallas_call x1, Pallas kernels, local(): pl.pallas_call(functools.partial(step_kernel, shards), out_shape=(pltpu.V...  143 us
    pallas_call x1, Pallas kernels, local(): pl.pallas_call(eject_kernel, out_shape=(full, half, half), in_specs=[pl.B...  3.36 us

profile of v7, /device:TPU:0, one launch (start us, length us, event | category | flops | bytes accessed | tf_op | source)
XLA Modules:
  0.0 146.7 jit_solution(18021609914726082612)
XLA Ops:
  0.6 142.7 %step.1 = (f32[32,16,2048]{2,1,0:T(8,128)S(1)}, bf16[32,16,2048]{2,1,0:T(8,128)(2,1)S(1)}, bf16[32,16,2048]{2,1,0:T(8,128)(2,1)S(1)}) custom-call(s32[2,4]{1,0:T(2,128)} %bitcast.12, f32[32,16,2048]{2,1,0:T(8,128)} %bitcast.8, bf16[32,16,2048]{2,1,0:T(8,128)(2,1)} %bitcast.9, bf16[32,16,2048]{2,1,0:T(8,128)(2,1)} %bitcast.10, bf16[32,16,2048]{2,1,0:T(8,128)(2,1)} %bitcast.11), custom_call_target="tpu_custom_call" | custom-call | tf_op jit(solution)/shard_map/step/pallas_call | solution.py:357
  143.4 3.4 %eject.1 = (f32[32,16,2048]{2,1,0:T(8,128)}, bf16[32,16,2048]{2,1,0:T(8,128)(2,1)}, bf16[32,16,2048]{2,1,0:T(8,128)(2,1)}) custom-call(f32[32,16,2048]{2,1,0:T(8,128)S(1)} %get-tuple-element.9.a, bf16[32,16,2048]{2,1,0:T(8,128)(2,1)S(1)} %get-tuple-element.10.b, bf16[32,16,2048]{2,1,0:T(8,128)(2,1)S(1)} %get-tuple-element.11.c), custom_call_target="tpu_custom_call" | custom-call | tf_op jit(solution)/shard_map/eject/pallas_call | solution.py:369
